TPU v7x, 512 devices: a whole 4x8x8 slice. The times are simulated.
512 devices in a mesh: row: 128 (over z, y, core), col: 4 (over x).
Axes of the slice: x: 4, y: 8, z: 8, core: 2. Of those that a mesh axis runs over, the one named last changes fastest.
Arguments:
- kernel_panel: float32 [65536, 512], P('row', 'col'), may hold values from -66 to 66, as said below
- kernel_slab: float32 [65536, 2048], P('row', 'col'), may hold values from -6 to 6
Outputs:
- factor_panel: float32 [65536, 512], P('row', 'col')
- schur_slab: float32 [65536, 2048], P('row', 'col')
Inputs may be any that keep to these rules, and one draw needn't show every extreme that they name: `kernel_panel`: the first 512 rows form a symmetric positive definite matrix whose smallest eigenvalue is 0.5 or more.
All inputs are finite; a program needn't handle non-finite values.
Results may differ from a plain program's by a relative error of at most 0.00011.
Values sent between devices are 32-bit elements; how exact they have to be, the bound alone decides.
No kernel may reach another device: no remote copies, remote signals or barrier semaphores. Data moves between devices by JAX's collectives and lax.ppermute only.
A program may use at most 64 MiB of HBM per device.

v0:
```python
import jax
import jax.numpy as jnp
from jax import lax
from jax.sharding import Mesh
from jax.sharding import PartitionSpec as P

ROW = ("row_0", "row_1", "row_2")


def from_root(array, axes, root):
    array = jnp.where(lax.axis_index(axes) == root, array, jnp.zeros_like(array))
    for axis in axes:
        array = lax.psum(array, axis)
    return array


def side_by_side(arrays, axis, dim, along):
    widths = [a.shape[along] for a in arrays]
    both = jnp.concatenate(arrays, axis=along)
    whole = lax.all_gather(both, axis, axis=dim, tiled=True)
    return tuple(jnp.split(whole, [sum(widths[:k]) for k in range(1, len(widths))], axis=along))


def broadcast(block, axis, owner):
    block = jnp.where(lax.axis_index(axis) == owner, block, jnp.zeros_like(block))
    return lax.psum(block, axis)


def lower_inverse(square):
    lower_factor = jnp.linalg.cholesky(square)
    identity = jnp.eye(square.shape[0], dtype=jnp.float32)
    return jax.scipy.linalg.solve_triangular(lower_factor, identity, lower=True)


def times_transpose(leading, trailing):
    return lax.dot_general(
        leading,
        trailing,
        (((1,), (1,)), ((), ())),
        precision=lax.Precision.HIGHEST,
        preferred_element_type=jnp.float32,
    )


def shards(kernel_panel, kernel_slab):
    rows_dev, block_size = kernel_panel.shape
    block_count = lax.axis_size("col")
    col_index = lax.axis_index("col")
    row_index = lax.axis_index(ROW)
    rows_count = lax.axis_size(ROW)
    span_count = kernel_slab.shape[1] // rows_dev
    global_rows = row_index * rows_dev + lax.iota(jnp.int32, rows_dev)
    panel_columns = lax.iota(jnp.int32, block_count * block_size)
    lower_mask = panel_columns[None, :] <= global_rows[:, None]
    leading_rows = from_root(kernel_panel, ROW, 0)
    whole_leading, rows_all = side_by_side((leading_rows, kernel_panel), "col", 1, 0)
    inverse = lower_inverse(whole_leading)
    lower_rows = jnp.where(lower_mask, times_transpose(rows_all, inverse), 0.0)
    factor = lax.dynamic_slice_in_dim(lower_rows, col_index * block_size, block_size, 1)
    owner_row = 1 + (col_index * span_count + 0) % (rows_count - 1)
    gathered = broadcast(lower_rows, ROW, owner_row)
    schur_out = kernel_slab - times_transpose(lower_rows, gathered)
    return (factor, schur_out)


def solution(mesh):
    torus = Mesh(
        mesh.devices.reshape(8, 8, 2, mesh.shape["col"]), ("row_0", "row_1", "row_2", "col")
    )
    in_specs = (P(ROW, "col"), P(ROW, "col"))
    out_specs = (P(ROW, "col"), P(ROW, "col"))
    return jax.shard_map(
        shards, mesh=torus, in_specs=in_specs, out_specs=out_specs, check_vma=False
    )
```

profile of v0, /device:TPU:30, one launch (start us, length us, event | category | flops | bytes accessed | tf_op | source)
XLA Modules:
  0.0 604.4 jit_solution(5982314419704561706)
XLA Ops:
  9.1 85.2 %all-reduce.6.cloned.1.call-done = f32[512,128]{0,1:T(8,128)} async-done(((f32[512,128]{0,1:T(8,128)}), f32[512,128]{0,1:T(8,128)}) %all-reduce.6.cloned.1.call-update) | async-done | bytes 262160 | tf_op jit(solution)/shard_map/psum | solution.py:13
  94.4 78.0 %all-reduce.8.cloned.1.call-done = f32[512,128]{0,1:T(8,128)} async-done(((f32[512,128]{0,1:T(8,128)}), f32[512,128]{0,1:T(8,128)}) %all-reduce.8.cloned.1.call-update) | async-done | bytes 262160 | tf_op jit(solution)/shard_map/psum | solution.py:13
  172.5 36.7 %all-reduce.10.cloned.1.call-done = f32[512,128]{0,1:T(8,128)} async-done(((f32[512,128]{0,1:T(8,128)}), f32[512,128]{0,1:T(8,128)}) %all-reduce.10.cloned.1.call-update) | async-done | bytes 262160 | tf_op jit(solution)/shard_map/psum | solution.py:13
  209.2 1.8 pad_maximum_fusion
  212.0 35.3 %all-gather.2.cloned.1.call-done = f32[1024,512]{0,1:T(8,128)} async-done(((f32[1024,128]{0,1:T(8,128)}), f32[1024,512]{0,1:T(8,128)}) %all-gather.2.cloned.1.call-update) | async-done | bytes 2097168 | tf_op jit(solution)/shard_map/all_gather | solution.py:20
  247.3 1.2 slice-done
  248.8 1.4 fusion.8
  250.3 11.7 %cholesky.104 = f32[128,128]{1,0:T(8,128)S(1)} custom-call(f32[128,128]{1,0:T(8,128)S(1)} %cholesky.266), custom_call_target="Cholesky" | custom-call | tf_op jit(solution)/shard_map/jit(cholesky)/cholesky | solution.py:30
  262.1 9.8 %custom-call.31 = f32[1,128,128]{1,2,0:T(8,128)S(1)} custom-call(f32[1,128,128]{2,1,0:T(8,128)S(1)} %get-tuple-element.29), custom_call_target="InvertDiagBlocksLowerTriangular" | custom-call | tf_op jit(solution)/shard_map/jit(cholesky)/cholesky | solution.py:30
  272.7 11.7 %cholesky.217 = f32[128,128]{1,0:T(8,128)S(1)} custom-call(f32[128,128]{1,0:T(8,128)S(1)} %cholesky.270), custom_call_target="Cholesky" | custom-call | tf_op jit(solution)/shard_map/jit(cholesky)/cholesky | solution.py:30
  284.4 10.0 %custom-call.32 = f32[1,128,128]{1,2,0:T(8,128)S(1)} custom-call(f32[1,128,128]{2,1,0:T(8,128)S(1)} %get-tuple-element.26), custom_call_target="InvertDiagBlocksLowerTriangular" | custom-call | tf_op jit(solution)/shard_map/jit(cholesky)/cholesky | solution.py:30
  295.1 11.7 %cholesky.238 = f32[128,128]{1,0:T(8,128)S(1)} custom-call(f32[128,128]{1,0:T(8,128)S(1)} %cholesky.275), custom_call_target="Cholesky" | custom-call | tf_op jit(solution)/shard_map/jit(cholesky)/cholesky | solution.py:30
  307.5 9.8 %custom-call.33 = f32[1,128,128]{1,2,0:T(8,128)S(1)} custom-call(f32[1,128,128]{2,1,0:T(8,128)S(1)} %get-tuple-element.23), custom_call_target="InvertDiagBlocksLowerTriangular" | custom-call | tf_op jit(solution)/shard_map/jit(cholesky)/cholesky | solution.py:30
  317.9 11.7 %cholesky.255 = f32[128,128]{1,0:T(8,128)S(1)} custom-call(f32[128,128]{1,0:T(8,128)S(1)} %convolution_subtract_fusion.6), custom_call_target="Cholesky" | custom-call | tf_op jit(solution)/shard_map/jit(cholesky)/cholesky | solution.py:30
  333.8 10.3 %while.1 = (s32[]{:T(128)}, f32[512,512]{1,0:T(8,128)S(1)}, s32[4,2]{0,1:T(2,128)S(1)}, f32[4,128,128]{2,1,0:T(8,128)}, s32[]{:T(128)}) while((s32[]{:T(128)}, f32[512,512]{1,0:T(8,128)S(1)}, s32[4,2]{0,1:T(2,128)S(1)}, f32[4,128,128]{2,1,0:T(8,128)}, s32[]{:T(128)}) %tuple.32), condition=%wide.while_cond, body=%wide.while_body.sunk | while | flops 2 | bytes 132705 | solution.py:32
  334.4 2.0 bitcast_dynamic-update-slice_fusion.2
  337.0 2.0 bitcast_dynamic-update-slice_fusion.2
  339.6 2.0 bitcast_dynamic-update-slice_fusion.2
  342.2 2.0 bitcast_dynamic-update-slice_fusion.2
  344.2 40.1 %custom-call.34 = f32[4,128,128]{1,2,0:T(8,128)S(1)} custom-call(f32[4,128,128]{2,1,0:T(8,128)} %get-tuple-element.9), custom_call_target="InvertDiagBlocksLowerTriangular" | custom-call | tf_op jit(solution)/shard_map/jit(_solve_triangular)/triangular_solve | solution.py:32
  384.3 1.1 fusion.19
  388.1 4.6 broadcast_select_fusion
  393.5 200.3 %all-reduce.12.cloned.1.call-done = f32[512,512]{1,0:T(8,128)} async-done(((f32[512,512]{1,0:T(8,128)}), f32[512,512]{1,0:T(8,128)}) %all-reduce.12.cloned.1.call-update) | async-done | bytes 1048592 | tf_op jit(solution)/shard_map/psum | solution.py:26
  593.8 4.1 convolution_subtract_fusion
  (57 shorter events, 13.6 us)
Async XLA Ops:
  7.2 87.1 %all-reduce.6.cloned.1.call-start = ((), (), s32[]{:S(2)}) async-start(), calls=%async_computation | async-start | bytes 524288 | tf_op jit(solution)/shard_map/psum | solution.py:13
  9.1 163.3 %all-reduce.8.cloned.1.call-start = ((), (), s32[]{:S(2)}) async-start(), calls=%async_computation.1 | async-start | bytes 524288 | tf_op jit(solution)/shard_map/psum | solution.py:13
  94.3 114.8 %all-reduce.10.cloned.1.call-start = ((), (), s32[]{:S(2)}) async-start(), calls=%async_computation.2 | async-start | bytes 524288 | tf_op jit(solution)/shard_map/psum | solution.py:13
  172.4 74.9 %all-gather.2.cloned.1.call-start = ((), (), s32[]{:S(2)}) async-start(), calls=%async_computation.3 | async-start | bytes 2621440 | tf_op jit(solution)/shard_map/all_gather | solution.py:20
  211.0 382.8 %all-reduce.12.cloned.1.call-start = ((), (), s32[]{:S(2)}) async-start(), calls=%async_computation.4 | async-start | bytes 2097152 | tf_op jit(solution)/shard_map/psum | solution.py:26
  247.3 1.2 slice-start
  385.7 2.4 copy-start
  388.1 205.7 %copy-start.1 = (f32[512,512]{1,0:T(8,128)S(1)}, f32[512,512]{1,0:T(8,128)}, u32[]{:S(2)}) copy-start(f32[512,512]{1,0:T(8,128)} %param.3) | copy-start | bytes 3145732
Sparse Core Ops, SparseCore 0:
  10.9 83.4 all-reduce.5
  96.6 75.7 all-reduce.7
  175.3 33.8 all-reduce.9
  211.7 35.5 all-gather.1
  392.8 200.9 all-reduce.11
where the time goes:
time: 605 us; the launch traced here: 604 us
  waiting for transfers between devices  436 us (72%)
  other arithmetic  124 us (20%)
  between operations  16.6 us (3%)
  matrix products  14.3 us (2%)
  local copies, waits for them, and re-layouts  13.8 us (2%)
    psum x1, waiting for transfers between devices, broadcast(): return lax.psum(block, axis)  200 us
    psum x3, waiting for transfers between devices, from_root(): array = lax.psum(array, axis)  200 us
    another operation x14, other arithmetic, lower_inverse(): lower_factor = jnp.linalg.cholesky(square)  78.7 us
    another operation x3, other arithmetic, lower_inverse(): return jax.scipy.linalg.solve_triangular(lower_factor, identity, lower=True)  40.3 us
    all_gather x1, waiting for transfers between devices, side_by_side(): whole = lax.all_gather(both, axis, axis=dim, tiled=True)  35.3 us
  transfers between devices with their start and end apart: 5, of which 5 were waited for; matrix products, arithmetic and copies ran while one was open for 0% of the time, Pallas kernels for 0%

commit v1 on v0

v1 whole, which is shorter than its diff:
```python
import jax
import jax.numpy as jnp
from jax import lax
from jax.experimental import pallas as pl
from jax.experimental.pallas import tpu as pltpu
from jax.sharding import Mesh
from jax.sharding import PartitionSpec as P

ROW = ("z", "y", "k")
PLANE = ("z", "y")
F32 = jnp.float32
BF16 = jnp.bfloat16
STRIP = 8
BLOCK = 128


def split3(x):
    high = x.astype(BF16).astype(F32)
    rest = x - high
    mid = rest.astype(BF16).astype(F32)
    return high, mid, rest - mid


def outer_update(left, right):
    l1, l2, l3 = split3(left)
    r1, r2, r3 = split3(right)
    lhs = jnp.concatenate([l1, l1, l2, l1, l3, l2], axis=0).astype(BF16)
    rhs = jnp.concatenate([r1, r2, r1, r3, r1, r2], axis=0).astype(BF16)
    return lax.dot_general(lhs, rhs, (((0,), (0,)), ((), ())), preferred_element_type=F32)


def mul_t(a, b):
    return lax.dot_general(
        a, b, (((1,), (1,)), ((), ())), precision=lax.Precision.HIGHEST, preferred_element_type=F32
    )


def factor_block(d):
    row = lax.broadcasted_iota(jnp.int32, (STRIP, BLOCK), 0)
    lane = lax.broadcasted_iota(jnp.int32, (STRIP, BLOCK), 1)
    lane_full = lax.broadcasted_iota(jnp.int32, (BLOCK, BLOCK), 1)
    for o in range(0, BLOCK, STRIP):
        s = d[o : o + STRIP, :]
        cols = [jnp.broadcast_to(s[:, o + m : o + m + 1], (STRIP, BLOCK)) for m in range(STRIP)]
        s = jnp.where((lane >= o) & (lane < o + STRIP), jnp.where(lane - o == row, 1.0, 0.0), s)
        for j in range(STRIP):
            scale = lax.rsqrt(jnp.broadcast_to(cols[j][j : j + 1, :], (STRIP, BLOCK)))
            lj = cols[j] * scale
            below = jnp.where(row > j, lj, 0.0)
            pivot = jnp.broadcast_to(s[j : j + 1, :], (STRIP, BLOCK)) * scale
            s = jnp.where(row == j, pivot, s - below * pivot)
            for m in range(j + 1, STRIP):
                cols[m] = cols[m] - below * jnp.broadcast_to(lj[m : m + 1, :], (STRIP, BLOCK))
        d[o : o + STRIP, :] = s
        n = o + STRIP
        if n < BLOCK:
            update = outer_update(jnp.where(lane >= n, s, 0.0), s)
            lf = lane_full[n:, :]
            d[n:, :] = jnp.where((lf >= o) & (lf < n), 0.0, d[n:, :]) - update[n:, :]


def kernel(idx, g, h, x0, x1, x2, x3, slab, factor, schur, a, far, x, d):
    core, col, row_start = idx[0], idx[1], idx[2]
    size = slab.shape[0]

    def unpack(low, high):
        for half, ref in ((0, low), (1, high)):
            for j in range(2):
                a[2 * half + j] = ref[:, j].reshape(size, BLOCK)
                far[2 * half + j] = ref[:, 2 + j].reshape(size, BLOCK)

    @pl.when(core == 0)
    def _():
        unpack(g, h)

    @pl.when(core != 0)
    def _():
        unpack(h, g)

    for s, ref in enumerate((x0, x1, x2, x3)):
        x[lax.rem(col - s + 4, 4)] = ref[...]

    blocks = size // BLOCK
    tri = lax.broadcasted_iota(jnp.int32, (BLOCK, BLOCK), 0) >= lax.broadcasted_iota(
        jnp.int32, (BLOCK, BLOCK), 1
    )
    for j in range(blocks):
        o = j * BLOCK
        n = o + BLOCK
        d[...] = a[j, o:n, :]
        factor_block(d)
        inverse = jnp.where(tri, d[...], 0.0)
        if j + 1 < blocks:
            below = mul_t(a[j, n:, :], inverse)
            for m in range(j + 1, blocks):
                lo = (m - j - 1) * BLOCK
                a[m, m * BLOCK :, :] = a[m, m * BLOCK :, :] - mul_t(below[lo:], below[lo : lo + BLOCK])
        for ref in (x, far):
            solved = mul_t(ref[j], inverse)
            ref[j] = solved
            for m in range(j + 1, blocks):
                lo = (m - j - 1) * BLOCK
                ref[m] = ref[m] - mul_t(solved, below[lo : lo + BLOCK])
    rows = row_start + lax.broadcasted_iota(jnp.int32, (size, BLOCK), 0)
    lanes = lax.broadcasted_iota(jnp.int32, (size, BLOCK), 1)
    total = slab[...]
    for j in range(blocks):
        x[j] = jnp.where(lanes + j * BLOCK <= rows, x[j], 0.0)
        total = total - mul_t(x[j], far[j])
    schur[...] = total
    factor[...] = x[col]


def run_kernel(idx, g, h, xs, slab):
    size = slab.shape[0]
    vmem = pl.BlockSpec(memory_space=pltpu.VMEM)
    return pl.pallas_call(
        kernel,
        out_shape=(
            jax.ShapeDtypeStruct((size, BLOCK), F32),
            jax.ShapeDtypeStruct((size, size), F32),
        ),
        in_specs=[pl.BlockSpec(memory_space=pltpu.SMEM)] + [vmem] * 7,
        out_specs=(vmem, vmem),
        scratch_shapes=[pltpu.VMEM((4, size, BLOCK), F32)] * 3 + [pltpu.VMEM((BLOCK, BLOCK), F32)],
        compiler_params=pltpu.CompilerParams(vmem_limit_bytes=24 << 20),
    )(idx, g, h, *xs, slab)


def ring(n, s):
    return [(i, (i + s) % n) for i in range(n)]


def plan(kernel_panel, kernel_slab):
    core, col = lax.axis_index("k"), lax.axis_index("x")
    row_start = lax.axis_index(ROW) * kernel_panel.shape[0]
    right = lax.ppermute(kernel_panel, "x", ring(4, 1))
    left = lax.ppermute(kernel_panel, "x", ring(4, 3))
    across = lax.ppermute(kernel_panel, "x", ring(4, 2))

    pieces = lax.all_to_all(kernel_panel.reshape(64, 8, BLOCK), PLANE, 0, 0, tiled=True)
    parcel = jnp.stack([jnp.stack([pieces[0], pieces[(1 + c) // 2]]) for c in range(4)])
    parcel = jnp.broadcast_to(parcel[None], (2, 4, 2, 8, BLOCK)).reshape(8, 2, 8, BLOCK)
    parcel = lax.all_to_all(parcel, ("k", "x"), 0, 0, tiled=True).reshape(2, 4, 2, 8, BLOCK)
    lead = lax.dynamic_slice_in_dim(parcel[0, :, 0], 2 * core, 2, 0)
    far = lax.dynamic_index_in_dim(parcel[:, :, 1], lax.rem(1 + col, 2), 0, keepdims=False)
    far = lax.dynamic_slice_in_dim(far, 2 * core, 2, 0)
    mine = jnp.concatenate([lead, far], axis=0)
    spread = jnp.broadcast_to(mine[None], (64, 4, 8, BLOCK))
    g = lax.all_to_all(spread, PLANE, 0, 0, tiled=True)
    h = lax.ppermute(g, "k", ring(2, 1))
    idx = jnp.stack([core, col, row_start]).astype(jnp.int32)
    return run_kernel(idx, g, h, (kernel_panel, right, across, left), kernel_slab)


def solution(mesh):
    torus = Mesh(mesh.devices.reshape(8, 8, 2, mesh.shape["col"]), ("z", "y", "k", "x"))
    spec = P(ROW, "x")
    return jax.shard_map(
        plan, mesh=torus, in_specs=(spec, spec), out_specs=(spec, spec), check_vma=False
    )
```

time: 605 us -> 133 us (0.22)
  the two profiles are of different devices: /device:TPU:30 before, /device:TPU:1 now
where the time goes in v1:
time: 133 us; the launch traced here: 132 us
  blocking collectives  62.1 us (47%)
  Pallas kernels  34.6 us (26%)
  starting transfers between devices  21 us (16%)
  waiting for transfers between devices  12.9 us (10%)
    pallas_call x1, Pallas kernels, run_kernel(): pl.pallas_call(kernel, out_shape=(jax.ShapeDtypeStruct((size, BLOCK), F32...  34.6 us
    all_to_all x1, blocking collectives, plan(): g = lax.all_to_all(spread, PLANE, 0, 0, tiled=True)  32.1 us
    all_to_all x1, blocking collectives, plan(): lax.all_to_all(kernel_panel.reshape(64, 8, BLOCK), PLANE, 0, 0, tiled=True)  30 us
    all_to_all x1, starting transfers between devices, plan(): lax.all_to_all(parcel, ('k', 'x'), 0, 0, tiled=True)  7.36 us
    ppermute x1, waiting for transfers between devices, plan(): right = lax.ppermute(kernel_panel, 'x', ring(4, 1))  5.98 us
    all_to_all x1, waiting for transfers between devices, plan(): lax.all_to_all(parcel, ('k', 'x'), 0, 0, tiled=True)  4.97 us
    ppermute x1, starting transfers between devices, plan(): h = lax.ppermute(g, 'k', ring(2, 1))  4.32 us
    ppermute x1, starting transfers between devices, plan(): left = lax.ppermute(kernel_panel, 'x', ring(4, 3))  4.01 us
  transfers between devices with their start and end apart: 5, of which 3 were waited for; matrix products, arithmetic and copies ran while one was open for 0% of the time, Pallas kernels for 0%

profile of v1, /device:TPU:1, one launch (start us, length us, event | category | flops | bytes accessed | tf_op | source)
XLA Modules:
  0.0 132.2 jit_solution(2981966152644394815)
XLA Ops:
  0.6 30.0 %all_to_all.15 = f32[64,8,128]{2,1,0:T(8,128)S(1)} all-to-all(f32[64,8,128]{2,1,0:T(8,128)} %bitcast.16), channel_id=1, replica_groups=mesh['z'=8,'y'=8,'k'=2,'x'=4] {'z','y'}, dimensions={0} | all-to-all | bytes 524288 | tf_op jit(solution)/shard_map/all_to_all | solution.py:141
  30.6 0.6 broadcast_in_dim.4
  31.3 7.4 %all-to-all-start.1 = ((f32[8,2,8,128]{3,2,1,0:T(8,128)}), f32[8,2,8,128]{3,2,1,0:T(8,128)S(1)}, u32[]{:S(2)}, u32[]{:S(2)}) async-start(f32[8,2,8,128]{3,2,1,0:T(8,128)} %bitcast.7), calls=%async_computation.1 | async-start | bytes 131072 | tf_op jit(solution)/shard_map/all_to_all | solution.py:144
  38.6 5.0 %all-to-all-done.1 = f32[8,2,8,128]{3,2,1,0:T(8,128)S(1)} async-done(((f32[8,2,8,128]{3,2,1,0:T(8,128)}), f32[8,2,8,128]{3,2,1,0:T(8,128)S(1)}, u32[]{:S(2)}, u32[]{:S(2)}) %all-to-all-start.1) | async-done | bytes 65568 | tf_op jit(solution)/shard_map/all_to_all | solution.py:144
  43.6 0.1 broadcast_in_dim.5
  43.7 0.0 copy-start.1
  43.8 0.0 copy-start
  43.8 32.1 %all_to_all.16.g = f32[64,4,8,128]{3,2,1,0:T(8,128)S(1)} all-to-all(f32[64,4,8,128]{3,2,1,0:T(8,128)S(1)} %broadcast_in_dim.5), channel_id=1, replica_groups=mesh['z'=8,'y'=8,'k'=2,'x'=4] {'z','y'}, dimensions={0} | all-to-all | bytes 2097152 | tf_op jit(solution)/shard_map/all_to_all | solution.py:150
  75.9 4.3 %collective-permute-start = (f32[64,4,8,128]{3,2,1,0:T(8,128)S(1)}, f32[64,4,8,128]{3,2,1,0:T(8,128)S(1)}, u32[]{:S(2)}, u32[]{:S(2)}) collective-permute-start(f32[64,4,8,128]{3,2,1,0:T(8,128)S(1)} %all_to_all.16.g), channel_id=1, source_target_pairs={{0,4},{4,0},{1,5},{5,1},{2,6},{6,2},{3,7},{7,3},{8,12},{12,8},{9,1... | collective-permute-start | bytes 3145736 | tf_op jit(solution)/shard_map/ppermute | solution.py:151
  80.2 0.0 copy-done.1
  80.2 2.8 %collective-permute-start.2 = (f32[512,128]{1,0:T(8,128)S(1)}, f32[512,128]{1,0:T(8,128)}, u32[]{:S(2)}, u32[]{:S(2)}) collective-permute-start(f32[512,128]{1,0:T(8,128)S(1)} %copy-done.1), channel_id=1, source_target_pairs={{0,2},{1,3},{2,0},{3,1},{4,6},{5,7},{6,4},{7,5},{8,10},{9,11},{10,... | collective-permute-start | bytes 786440 | tf_op jit(solution)/shard_map/ppermute | solution.py:139
  83.0 2.5 %collective-permute-start.1 = (f32[512,128]{1,0:T(8,128)S(1)}, f32[512,128]{1,0:T(8,128)}, u32[]{:S(2)}, u32[]{:S(2)}) collective-permute-start(f32[512,128]{1,0:T(8,128)S(1)} %copy-done.1), channel_id=1, source_target_pairs={{0,1},{1,2},{2,3},{3,0},{4,5},{5,6},{6,7},{7,4},{8,9},{9,10},{10,1... | collective-permute-start | bytes 786440 | tf_op jit(solution)/shard_map/ppermute | solution.py:137
  85.5 4.0 %collective-permute-start.3 = (f32[512,128]{1,0:T(8,128)S(1)}, f32[512,128]{1,0:T(8,128)}, u32[]{:S(2)}, u32[]{:S(2)}) collective-permute-start(f32[512,128]{1,0:T(8,128)S(1)} %copy-done.1), channel_id=1, source_target_pairs={{0,3},{1,0},{2,1},{3,2},{4,7},{5,4},{6,5},{7,6},{8,11},{9,8},{10,9... | collective-permute-start | bytes 786440 | tf_op jit(solution)/shard_map/ppermute | solution.py:138
  89.5 0.1 pad_add_fusion.idx
  89.6 2.0 %collective-permute-done.2.x2 = f32[512,128]{1,0:T(8,128)} collective-permute-done((f32[512,128]{1,0:T(8,128)S(1)}, f32[512,128]{1,0:T(8,128)}, u32[]{:S(2)}, u32[]{:S(2)}) %collective-permute-start.2) | collective-permute-done | bytes 262176 | tf_op jit(solution)/shard_map/ppermute | solution.py:139
  91.6 6.0 %collective-permute-done.1.x1 = f32[512,128]{1,0:T(8,128)} collective-permute-done((f32[512,128]{1,0:T(8,128)S(1)}, f32[512,128]{1,0:T(8,128)}, u32[]{:S(2)}, u32[]{:S(2)}) %collective-permute-start.1) | collective-permute-done | bytes 262176 | tf_op jit(solution)/shard_map/ppermute | solution.py:137
  97.6 0.0 collective-permute-done.3.x3
  97.6 0.0 collective-permute-done.h
  97.6 0.0 copy-done
  97.6 34.6 %shard_map.41 = (f32[512,128]{1,0:T(8,128)}, f32[512,512]{1,0:T(8,128)}) custom-call(s32[3]{0:T(128)S(1)} %pad_add_fusion.idx, f32[64,4,8,128]{3,2,1,0:T(8,128)S(1)} %all_to_all.16.g, f32[64,4,8,128]{3,2,1,0:T(8,128)S(1)} %collective-permute-done.h, f32[512,128]{1,0:T(8,128)S(1)} %copy-done.1, f32[512,128]{1,0:T(8,128)} %collective-permute-done.1.x1, ...), custom_call_target="tpu_custom_call" | custom-call | tf_op jit(solution)/shard_map/pallas_call | solution.py:117
  (8 shorter events, 0.0 us)
Async XLA Ops:
  31.3 12.3 %all-to-all-start.1 = ((f32[8,2,8,128]{3,2,1,0:T(8,128)}), f32[8,2,8,128]{3,2,1,0:T(8,128)S(1)}, u32[]{:S(2)}, u32[]{:S(2)}) async-start(f32[8,2,8,128]{3,2,1,0:T(8,128)} %bitcast.7), calls=%async_computation.1 | async-start | bytes 131072 | tf_op jit(solution)/shard_map/all_to_all | solution.py:144
  43.7 36.5 %copy-start.1 = (f32[512,128]{1,0:T(8,128)S(1)}, f32[512,128]{1,0:T(8,128)}, u32[]{:S(2)}) copy-start(f32[512,128]{1,0:T(8,128)} %x0.1) | copy-start | bytes 786436
  43.8 53.8 %copy-start = (f32[512,512]{1,0:T(8,128)S(1)}, f32[512,512]{1,0:T(8,128)}, u32[]{:S(2)}) copy-start(f32[512,512]{1,0:T(8,128)} %slab.1) | copy-start | bytes 3145732
  75.9 21.7 %collective-permute-start = (f32[64,4,8,128]{3,2,1,0:T(8,128)S(1)}, f32[64,4,8,128]{3,2,1,0:T(8,128)S(1)}, u32[]{:S(2)}, u32[]{:S(2)}) collective-permute-start(f32[64,4,8,128]{3,2,1,0:T(8,128)S(1)} %all_to_all.16.g), channel_id=1, source_target_pairs={{0,4},{4,0},{1,5},{5,1},{2,6},{6,2},{3,7},{7,3},{8,12},{12,8},{9,1... | collective-permute-start | bytes 3145736 | tf_op jit(solution)/shard_map/ppermute | solution.py:151
  80.2 11.4 %collective-permute-start.2 = (f32[512,128]{1,0:T(8,128)S(1)}, f32[512,128]{1,0:T(8,128)}, u32[]{:S(2)}, u32[]{:S(2)}) collective-permute-start(f32[512,128]{1,0:T(8,128)S(1)} %copy-done.1), channel_id=1, source_target_pairs={{0,2},{1,3},{2,0},{3,1},{4,6},{5,7},{6,4},{7,5},{8,10},{9,11},{10,... | collective-permute-start | bytes 786440 | tf_op jit(solution)/shard_map/ppermute | solution.py:139
  83.0 14.6 %collective-permute-start.1 = (f32[512,128]{1,0:T(8,128)S(1)}, f32[512,128]{1,0:T(8,128)}, u32[]{:S(2)}, u32[]{:S(2)}) collective-permute-start(f32[512,128]{1,0:T(8,128)S(1)} %copy-done.1), channel_id=1, source_target_pairs={{0,1},{1,2},{2,3},{3,0},{4,5},{5,6},{6,7},{7,4},{8,9},{9,10},{10,1... | collective-permute-start | bytes 786440 | tf_op jit(solution)/shard_map/ppermute | solution.py:137
  85.5 12.1 %collective-permute-start.3 = (f32[512,128]{1,0:T(8,128)S(1)}, f32[512,128]{1,0:T(8,128)}, u32[]{:S(2)}, u32[]{:S(2)}) collective-permute-start(f32[512,128]{1,0:T(8,128)S(1)} %copy-done.1), channel_id=1, source_target_pairs={{0,3},{1,0},{2,1},{3,2},{4,7},{5,4},{6,5},{7,6},{8,11},{9,8},{10,9... | collective-permute-start | bytes 786440 | tf_op jit(solution)/shard_map/ppermute | solution.py:138

commit v2 on v1

v2 whole, which is shorter than its diff:
```python
import jax
import jax.numpy as jnp
from jax import lax
from jax.experimental import pallas as pl
from jax.experimental.pallas import tpu as pltpu
from jax.sharding import Mesh
from jax.sharding import PartitionSpec as P

ROW = ("z", "y", "k")
PLANE = ("z", "y")
F32 = jnp.float32
BF16 = jnp.bfloat16
STRIP = 8
BLOCK = 128
STRIPS = BLOCK // STRIP
AHEAD = 3


def split3(x):
    high = x.astype(BF16).astype(F32)
    rest = x - high
    mid = rest.astype(BF16).astype(F32)
    return high, mid, rest - mid


def outer_update(left, right):
    l1, l2, l3 = split3(left)
    r1, r2, r3 = split3(right)
    lhs = jnp.concatenate([l1, l1, l2, l1, l3, l2], axis=0).astype(BF16)
    rhs = jnp.concatenate([r1, r2, r1, r3, r1, r2], axis=0).astype(BF16)
    return lax.dot_general(lhs, rhs, (((0,), (0,)), ((), ())), preferred_element_type=F32)


def mul_t(a, b):
    return lax.dot_general(
        a, b, (((1,), (1,)), ((), ())), precision=lax.Precision.HIGHEST, preferred_element_type=F32
    )


def mul_t3(a, b):
    a1, b1 = a.astype(BF16), b.astype(BF16)
    a2, b2 = (a - a1.astype(F32)).astype(BF16), (b - b1.astype(F32)).astype(BF16)

    def dot(left, right):
        return lax.dot_general(left, right, (((1,), (1,)), ((), ())), preferred_element_type=F32)

    return dot(a1, b1) + (dot(a1, b2) + dot(a2, b1))


def over_lanes(x, lane):
    return jnp.broadcast_to(x[:, lane : lane + 1], (STRIP, BLOCK))


def over_rows(x, r):
    return jnp.broadcast_to(x[r : r + 1, :], (STRIP, BLOCK))


def factor_block(load, store):
    row = lax.broadcasted_iota(jnp.int32, (STRIP, BLOCK), 0)
    lane = lax.broadcasted_iota(jnp.int32, (STRIP, BLOCK), 1)
    rows = [load(t) for t in range(STRIPS)]
    spread = {}
    for b in range(STRIPS):
        o = b * STRIP
        window = range(b, min(b + AHEAD + 1, STRIPS))
        below = window[1:]
        inside = (lane >= o) & (lane < o + STRIP)
        now = {t: spread.get(t) or [over_lanes(rows[t], o + m) for m in range(STRIP)] for t in window}
        later = {t: [over_lanes(rows[t], o + STRIP + m) for m in range(STRIP)] for t in below}
        unit = jnp.where(lane - o == row, 1.0, 0.0)
        strip = {t: jnp.where(inside, unit if t == b else 0.0, rows[t]) for t in window}
        for j in range(STRIP):
            scale = lax.rsqrt(over_rows(now[b][j], j))
            column = now[b][j] * scale
            across = {m: over_rows(column, m) for m in range(j + 1, STRIP)}
            for m in across:
                now[b][m] = now[b][m] - column * across[m]
            pivot = over_rows(strip[b], j) * scale
            reduced = strip[b] - jnp.where(row > j, column, 0.0) * pivot
            strip[b] = jnp.where(row == j, pivot, reduced)
            across_next = None
            for t in below:
                column = now[t][j] * scale
                strip[t] = strip[t] - column * pivot
                for m in across:
                    now[t][m] = now[t][m] - column * across[m]
                if t == b + 1:
                    across_next = [over_rows(column, m) for m in range(STRIP)]
                for m in range(STRIP):
                    later[t][m] = later[t][m] - column * across_next[m]
        for t in window:
            rows[t] = strip[t]
        store(b, strip[b])
        spread = later
        n = b + AHEAD + 1
        if n < STRIPS:
            update = outer_update(jnp.where(lane >= n * STRIP, strip[b], 0.0), strip[b])
            for t in range(n, STRIPS):
                rows[t] = jnp.where(inside, 0.0, rows[t]) - update[t * STRIP : (t + 1) * STRIP]


def unpack(core, mine, other, out):
    size = out.shape[1]

    def place(low, high):
        for half, ref in ((0, low), (1, high)):
            for j in range(2):
                out[2 * half + j] = ref[:, j].reshape(size, BLOCK)

    @pl.when(core == 0)
    def _():
        place(mine, other)

    @pl.when(core != 0)
    def _():
        place(other, mine)


def place_of(row_block, col_block):
    return row_block * (row_block - 1) // 2 + col_block


def factor_kernel(idx, mine, other, inverse, lower, a, d):
    blocks = a.shape[0]
    unpack(idx[0], mine, other, a)
    tri = lax.broadcasted_iota(jnp.int32, (BLOCK, BLOCK), 0) >= lax.broadcasted_iota(
        jnp.int32, (BLOCK, BLOCK), 1
    )
    for j in range(blocks):
        o = j * BLOCK
        n = o + BLOCK

        def load(t, j=j, o=o):
            return a[j, o + t * STRIP : o + (t + 1) * STRIP, :]

        def store(t, value):
            d[t * STRIP : (t + 1) * STRIP, :] = value

        factor_block(load, store)
        inv = jnp.where(tri, d[...], 0.0)
        inverse[j] = inv
        if j + 1 < blocks:
            below = mul_t(a[j, n:, :], inv)
            for m in range(j + 1, blocks):
                lo = (m - j - 1) * BLOCK
                s = m * BLOCK
                lower[place_of(m, j)] = below[lo : lo + BLOCK]
                a[m, s:, :] = a[m, s:, :] - mul_t(below[lo:], below[lo : lo + BLOCK])


def solve(x, inverse, lower):
    blocks = x.shape[0]
    for j in range(blocks):
        solved = mul_t(x[j], inverse[j])
        x[j] = solved
        for m in range(j + 1, blocks):
            x[m] = x[m] - mul_t(solved, lower[place_of(m, j)])


def own_kernel(idx, own0, own1, own2, own3, inverse, lower, out, factor):
    col, row_start = idx[1], idx[2]
    blocks, size = out.shape[0], out.shape[1]
    for shift, ref in enumerate((own0, own1, own2, own3)):
        out[lax.rem(col - shift + blocks, blocks)] = ref[...]
    solve(out, inverse, lower)
    rows = row_start + lax.broadcasted_iota(jnp.int32, (size, BLOCK), 0)
    lanes = lax.broadcasted_iota(jnp.int32, (size, BLOCK), 1)
    for j in range(blocks):
        out[j] = jnp.where(lanes + j * BLOCK <= rows, out[j], 0.0)
    factor[...] = out[col]


def schur_kernel(idx, own, mine, other, inverse, lower, slab, schur, far):
    unpack(idx[0], mine, other, far)
    solve(far, inverse, lower)
    total = slab[...]
    for j in range(far.shape[0]):
        total = total - mul_t3(own[j], far[j])
    schur[...] = total


def call(body, outs, flops, scratch, *args):
    vmem = pl.BlockSpec(memory_space=pltpu.VMEM)
    bytes_accessed = sum(4 * a.size for a in args) + sum(4 * o.size for o in outs)
    return pl.pallas_call(
        body,
        out_shape=outs,
        in_specs=[pl.BlockSpec(memory_space=pltpu.SMEM)] + [vmem] * (len(args) - 1),
        out_specs=tuple(vmem for _ in outs),
        scratch_shapes=[pltpu.VMEM(s, F32) for s in scratch],
        compiler_params=pltpu.CompilerParams(vmem_limit_bytes=16 << 20),
        cost_estimate=pl.CostEstimate(
            flops=flops, bytes_accessed=bytes_accessed, transcendentals=0
        ),
    )(*args)


def plan(kernel_panel, kernel_slab):
    size = kernel_panel.shape[0]
    core, col = lax.axis_index("k"), lax.axis_index("x")
    row_start = lax.axis_index(ROW) * size
    idx = jnp.stack([core, col, row_start]).astype(jnp.int32)

    pieces = lax.all_to_all(kernel_panel.reshape(64, 8, BLOCK), PLANE, 0, 0, tiled=True)
    parcel = jnp.stack([jnp.stack([pieces[0], pieces[(1 + c) // 2]]) for c in range(4)])
    parcel = jnp.broadcast_to(parcel[None], (2, 4, 2, 8, BLOCK)).reshape(8, 2, 8, BLOCK)
    parcel = lax.all_to_all(parcel, ("k", "x"), 0, 0, tiled=True).reshape(2, 4, 2, 8, BLOCK)
    lead = lax.dynamic_slice_in_dim(parcel[0, :, 0], 2 * core, 2, 0)
    far = lax.dynamic_index_in_dim(parcel[:, :, 1], lax.rem(1 + col, 2), 0, keepdims=False)
    far = lax.dynamic_slice_in_dim(far, 2 * core, 2, 0)

    def spread(piece):
        copies = jnp.broadcast_to(piece[None], (64, 2, 8, BLOCK))
        return lax.all_to_all(copies, PLANE, 0, 0, tiled=True)

    lead = spread(lead)
    lead_other = lax.ppermute(lead, "k", [(0, 1), (1, 0)])
    far = spread(far)
    own = [kernel_panel]
    for shift in (1, 2, 3):
        own.append(lax.ppermute(kernel_panel, "x", [(i, (i + shift) % 4) for i in range(4)]))
    blocks = jax.ShapeDtypeStruct((4, size, BLOCK), F32)
    inverse, lower = call(
        factor_kernel,
        (
            jax.ShapeDtypeStruct((4, BLOCK, BLOCK), F32),
            jax.ShapeDtypeStruct((6, BLOCK, BLOCK), F32),
        ),
        2 * 10**10,
        [(4, size, BLOCK), (BLOCK, BLOCK)],
        idx,
        lead,
        lead_other,
    )
    far_other = lax.ppermute(far, "k", [(0, 1), (1, 0)])
    own, factor = call(
        own_kernel,
        (blocks, jax.ShapeDtypeStruct((size, BLOCK), F32)),
        2 * 10**9,
        [],
        idx,
        *own,
        inverse,
        lower,
    )
    (schur,) = call(
        schur_kernel,
        (jax.ShapeDtypeStruct((size, size), F32),),
        4 * 10**9,
        [(4, size, BLOCK)],
        idx,
        own,
        far,
        far_other,
        inverse,
        lower,
        kernel_slab,
    )
    return factor, schur


def solution(mesh):
    torus = Mesh(mesh.devices.reshape(8, 8, 2, mesh.shape["col"]), ("z", "y", "k", "x"))
    spec = P(ROW, "x")
    return jax.shard_map(
        plan, mesh=torus, in_specs=(spec, spec), out_specs=(spec, spec), check_vma=False
    )
```

time: 133 us -> 122 us (0.917)
  blocking collectives: 62.1 us -> 30 us
  starting transfers between devices: 21 us -> 36.3 us
  waiting for transfers between devices: 12.9 us -> 27.3 us
  Pallas kernels: 34.6 us -> 24.2 us
  local copies, waits for them, and re-layouts: 0.78 us -> 2.33 us
    all_to_all x1 -> x0, blocking collectives: 32.1 us -> none  [plan(): g = lax.all_to_all(spread, PLANE, 0, 0, tiled=True)]
    all_to_all x0 -> x2, waiting for transfers between devices: none -> 22.3 us  [spread(): return lax.all_to_all(copies, PLANE, 0, 0, tiled=True)]
    all_to_all x0 -> x2, starting transfers between devices: none -> 11.1 us  [spread(): return lax.all_to_all(copies, PLANE, 0, 0, tiled=True)]
    pallas_call x1 -> x3, Pallas kernels: 34.6 us -> 24.2 us  [call(): pl.pallas_call(body, out_shape=outs, in_specs=[pl.BlockSpec(memory_space=...]
    ppermute x4 -> x5, waiting for transfers between devices: 7.98 us -> 0.01 us  [the longest x3 0.01 us: plan(): lax.ppermute(kernel_panel, 'x', [(i, (i + shift) % 4) for i in range(4)])]
    ppermute x4 -> x5, starting transfers between devices: 13.6 us -> 17.8 us  [the longest x3 8.68 us: plan(): lax.ppermute(kernel_panel, 'x', [(i, (i + shift) % 4) for i in range(4)])]
    broadcast_in_dim x1 -> x4, local copies, waits for them, and re-layouts: 0.12 us -> 1.67 us  [spread(): copies = jnp.broadcast_to(piece[None], (64, 2, 8, BLOCK))]
  transfers between devices with their start and end apart: 5 -> 8, of which waited for: 3 -> 3; matrix products, arithmetic and copies ran while one was open for 0% -> 0% of each run, Pallas kernels for 0% -> 14%
where the time goes in v2:
time: 122 us; the launch traced here: 121 us
  starting transfers between devices  36.3 us (30%)
  blocking collectives  30 us (25%)
  waiting for transfers between devices  27.3 us (22%)
  Pallas kernels  24.2 us (20%)
  local copies, waits for them, and re-layouts  2.33 us (2%)
    all_to_all x1, blocking collectives, plan(): lax.all_to_all(kernel_panel.reshape(64, 8, BLOCK), PLANE, 0, 0, tiled=True)  30 us
    pallas_call x3, Pallas kernels, call(): pl.pallas_call(body, out_shape=outs, in_specs=[pl.BlockSpec(memory_space=...  24.2 us
    all_to_all x2, waiting for transfers between devices, spread(): return lax.all_to_all(copies, PLANE, 0, 0, tiled=True)  22.3 us
    all_to_all x2, starting transfers between devices, spread(): return lax.all_to_all(copies, PLANE, 0, 0, tiled=True)  11.1 us
    ppermute x3, starting transfers between devices, plan(): lax.ppermute(kernel_panel, 'x', [(i, (i + shift) % 4) for i in range(4)])  8.68 us
    all_to_all x1, starting transfers between devices, plan(): lax.all_to_all(parcel, ('k', 'x'), 0, 0, tiled=True)  7.36 us
    ppermute x1, starting transfers between devices, plan(): far_other = lax.ppermute(far, 'k', [(0, 1), (1, 0)])  5.8 us
    all_to_all x1, waiting for transfers between devices, plan(): lax.all_to_all(parcel, ('k', 'x'), 0, 0, tiled=True)  4.97 us
  transfers between devices with their start and end apart: 8, of which 3 were waited for; matrix products, arithmetic and copies ran while one was open for 0% of the time, Pallas kernels for 14%

profile of v2, /device:TPU:1, one launch (start us, length us, event | category | flops | bytes accessed | tf_op | source)
XLA Modules:
  0.0 121.0 jit_solution(11049139004409607461)
XLA Ops:
  0.6 30.0 %all_to_all.20 = f32[64,8,128]{2,1,0:T(8,128)S(1)} all-to-all(f32[64,8,128]{2,1,0:T(8,128)} %bitcast.16), channel_id=1, replica_groups=mesh['z'=8,'y'=8,'k'=2,'x'=4] {'z','y'}, dimensions={0} | all-to-all | bytes 524288 | tf_op jit(solution)/shard_map/all_to_all | solution.py:204
  30.6 0.6 broadcast_in_dim.10
  31.3 7.4 %all-to-all-start.1 = ((f32[8,2,8,128]{3,2,1,0:T(8,128)}), f32[8,2,8,128]{3,2,1,0:T(8,128)S(1)}, u32[]{:S(2)}, u32[]{:S(2)}) async-start(f32[8,2,8,128]{3,2,1,0:T(8,128)} %bitcast.7), calls=%async_computation.1 | async-start | bytes 131072 | tf_op jit(solution)/shard_map/all_to_all | solution.py:207
  38.6 5.0 %all-to-all-done.1 = f32[8,2,8,128]{3,2,1,0:T(8,128)S(1)} async-done(((f32[8,2,8,128]{3,2,1,0:T(8,128)}), f32[8,2,8,128]{3,2,1,0:T(8,128)S(1)}, u32[]{:S(2)}, u32[]{:S(2)}) %all-to-all-start.1) | async-done | bytes 65568 | tf_op jit(solution)/shard_map/all_to_all | solution.py:207
  43.6 0.8 broadcast_in_dim.24
  44.4 4.6 %all-to-all-start.2 = ((f32[64,2,8,128]{3,2,1,0:T(8,128)}), f32[64,2,8,128]{3,2,1,0:T(8,128)S(1)}, u32[]{:S(2)}, u32[]{:S(2)}) async-start(f32[64,2,8,128]{3,2,1,0:T(8,128)} %broadcast_in_dim.24), calls=%async_computation.2 | async-start | bytes 1048576 | tf_op jit(solution)/shard_map/all_to_all | solution.py:214
  49.1 17.8 %all-to-all-done.2.mine = f32[64,2,8,128]{3,2,1,0:T(8,128)S(1)} async-done(((f32[64,2,8,128]{3,2,1,0:T(8,128)}), f32[64,2,8,128]{3,2,1,0:T(8,128)S(1)}, u32[]{:S(2)}, u32[]{:S(2)}) %all-to-all-start.2) | async-done | bytes 524320 | tf_op jit(solution)/shard_map/all_to_all | solution.py:214
  67.0 0.8 broadcast_in_dim.26
  67.8 6.5 %all-to-all-start.3 = ((f32[64,2,8,128]{3,2,1,0:T(8,128)}), f32[64,2,8,128]{3,2,1,0:T(8,128)S(1)}, u32[]{:S(2)}, u32[]{:S(2)}) async-start(f32[64,2,8,128]{3,2,1,0:T(8,128)} %broadcast_in_dim.26), calls=%async_computation.3 | async-start | bytes 1048576 | tf_op jit(solution)/shard_map/all_to_all | solution.py:214
  74.3 3.3 %collective-permute-start.3 = (f32[64,2,8,128]{3,2,1,0:T(8,128)S(1)}, f32[64,2,8,128]{3,2,1,0:T(8,128)S(1)}, u32[]{:S(2)}, u32[]{:S(2)}) collective-permute-start(f32[64,2,8,128]{3,2,1,0:T(8,128)S(1)} %all-to-all-done.2.mine), channel_id=1, source_target_pairs={{0,4},{4,0},{1,5},{5,1},{2,6},{6,2},{3,7},{7,3},{8,12},{12,8},{9,1... | collective-permute-start | bytes 1572872 | tf_op jit(solution)/shard_map/ppermute | solution.py:217
  77.6 2.4 %collective-permute-start = (f32[512,128]{1,0:T(8,128)S(1)}, f32[512,128]{1,0:T(8,128)S(1)}, u32[]{:S(2)}, u32[]{:S(2)}) collective-permute-start(f32[512,128]{1,0:T(8,128)S(1)} %copy-done), channel_id=1, source_target_pairs={{0,1},{1,2},{2,3},{3,0},{4,5},{5,6},{6,7},{7,4},{8,9},{9,10},{10,1... | collective-permute-start | bytes 786440 | tf_op jit(solution)/shard_map/ppermute | solution.py:221
  80.0 3.4 %collective-permute-start.1 = (f32[512,128]{1,0:T(8,128)S(1)}, f32[512,128]{1,0:T(8,128)S(1)}, u32[]{:S(2)}, u32[]{:S(2)}) collective-permute-start(f32[512,128]{1,0:T(8,128)S(1)} %copy-done), channel_id=1, source_target_pairs={{0,2},{1,3},{2,0},{3,1},{4,6},{5,7},{6,4},{7,5},{8,10},{9,11},{10,... | collective-permute-start | bytes 786440 | tf_op jit(solution)/shard_map/ppermute | solution.py:221
  83.5 2.9 %collective-permute-start.2 = (f32[512,128]{1,0:T(8,128)S(1)}, f32[512,128]{1,0:T(8,128)S(1)}, u32[]{:S(2)}, u32[]{:S(2)}) collective-permute-start(f32[512,128]{1,0:T(8,128)S(1)} %copy-done), channel_id=1, source_target_pairs={{0,3},{1,0},{2,1},{3,2},{4,7},{5,4},{6,5},{7,6},{8,11},{9,8},{10,9... | collective-permute-start | bytes 786440 | tf_op jit(solution)/shard_map/ppermute | solution.py:221
  86.3 0.1 pad_add_fusion.idx
  86.4 4.5 %all-to-all-done.3.mine = f32[64,2,8,128]{3,2,1,0:T(8,128)S(1)} async-done(((f32[64,2,8,128]{3,2,1,0:T(8,128)}), f32[64,2,8,128]{3,2,1,0:T(8,128)S(1)}, u32[]{:S(2)}, u32[]{:S(2)}) %all-to-all-start.3) | async-done | bytes 524320 | tf_op jit(solution)/shard_map/all_to_all | solution.py:214
  90.9 5.8 %collective-permute-start.4 = (f32[64,2,8,128]{3,2,1,0:T(8,128)S(1)}, f32[64,2,8,128]{3,2,1,0:T(8,128)S(1)}, u32[]{:S(2)}, u32[]{:S(2)}) collective-permute-start(f32[64,2,8,128]{3,2,1,0:T(8,128)S(1)} %all-to-all-done.3.mine), channel_id=1, source_target_pairs={{0,4},{4,0},{1,5},{5,1},{2,6},{6,2},{3,7},{7,3},{8,12},{12,8},{9,1... | collective-permute-start | bytes 1572872 | tf_op jit(solution)/shard_map/ppermute | solution.py:235
  96.7 0.0 collective-permute-done.3.other
  96.8 12.4 %shard_map.41 = (f32[4,128,128]{2,1,0:T(8,128)S(1)}, f32[6,128,128]{2,1,0:T(8,128)S(1)}) custom-call(s32[3]{0:T(128)S(1)} %pad_add_fusion.idx, f32[64,2,8,128]{3,2,1,0:T(8,128)S(1)} %all-to-all-done.2.mine, f32[64,2,8,128]{3,2,1,0:T(8,128)S(1)} %collective-permute-done.3.other), custom_call_target="tpu_custom_call" | custom-call | flops 20000000000 | bytes 1703948 | tf_op jit(solution)/shard_map/pallas_call | solution.py:185
  109.2 0.0 collective-permute-done.own1
  109.2 0.0 collective-permute-done.1.own2
  109.2 0.0 copy-start.1
  109.2 5.0 %shard_map.42 = (f32[4,512,128]{2,1,0:T(8,128)S(1)}, f32[512,128]{1,0:T(8,128)}) custom-call(s32[3]{0:T(128)S(1)} %pad_add_fusion.idx, f32[512,128]{1,0:T(8,128)S(1)} %copy-done, f32[512,128]{1,0:T(8,128)S(1)} %collective-permute-done.own1, f32[512,128]{1,0:T(8,128)S(1)} %collective-permute-done.1.own2, f32[512,128]{1,0:T(8,128)S(1)} %collective-permute-done.2.own3, ...), custom_call_target="tpu_custom_call" | custom-call | flops 2000000000 | bytes 3014668 | tf_op jit(solution)/shard_map/pallas_call | solution.py:185
  114.2 0.0 collective-permute-done.4.other
  114.3 6.8 %shard_map.43 = f32[512,512]{1,0:T(8,128)} custom-call(s32[3]{0:T(128)S(1)} %pad_add_fusion.idx, f32[4,512,128]{2,1,0:T(8,128)S(1)} %get-tuple-element.9.own, f32[64,2,8,128]{3,2,1,0:T(8,128)S(1)} %all-to-all-done.3.mine, f32[64,2,8,128]{3,2,1,0:T(8,128)S(1)} %collective-permute-done.4.other, f32[4,128,128]{2,1,0:T(8,128)S(1)} %get-tuple-element.6.inverse, ...), custom_call_target="tpu_custom_call" | custom-call | flops 4000000000 | bytes 4849676 | tf_op jit(solution)/shard_map/pallas_call | solution.py:185
  (11 shorter events, 0.0 us)
Async XLA Ops:
  31.3 12.3 %all-to-all-start.1 = ((f32[8,2,8,128]{3,2,1,0:T(8,128)}), f32[8,2,8,128]{3,2,1,0:T(8,128)S(1)}, u32[]{:S(2)}, u32[]{:S(2)}) async-start(f32[8,2,8,128]{3,2,1,0:T(8,128)} %bitcast.7), calls=%async_computation.1 | async-start | bytes 131072 | tf_op jit(solution)/shard_map/all_to_all | solution.py:207
  44.4 22.5 %all-to-all-start.2 = ((f32[64,2,8,128]{3,2,1,0:T(8,128)}), f32[64,2,8,128]{3,2,1,0:T(8,128)S(1)}, u32[]{:S(2)}, u32[]{:S(2)}) async-start(f32[64,2,8,128]{3,2,1,0:T(8,128)} %broadcast_in_dim.24), calls=%async_computation.2 | async-start | bytes 1048576 | tf_op jit(solution)/shard_map/all_to_all | solution.py:214
  67.8 9.8 %copy-start = (f32[512,128]{1,0:T(8,128)S(1)}, f32[512,128]{1,0:T(8,128)}, u32[]{:S(2)}) copy-start(f32[512,128]{1,0:T(8,128)} %own0.1) | copy-start | bytes 786436
  67.8 23.1 %all-to-all-start.3 = ((f32[64,2,8,128]{3,2,1,0:T(8,128)}), f32[64,2,8,128]{3,2,1,0:T(8,128)S(1)}, u32[]{:S(2)}, u32[]{:S(2)}) async-start(f32[64,2,8,128]{3,2,1,0:T(8,128)} %broadcast_in_dim.26), calls=%async_computation.3 | async-start | bytes 1048576 | tf_op jit(solution)/shard_map/all_to_all | solution.py:214
  74.3 22.5 %collective-permute-start.3 = (f32[64,2,8,128]{3,2,1,0:T(8,128)S(1)}, f32[64,2,8,128]{3,2,1,0:T(8,128)S(1)}, u32[]{:S(2)}, u32[]{:S(2)}) collective-permute-start(f32[64,2,8,128]{3,2,1,0:T(8,128)S(1)} %all-to-all-done.2.mine), channel_id=1, source_target_pairs={{0,4},{4,0},{1,5},{5,1},{2,6},{6,2},{3,7},{7,3},{8,12},{12,8},{9,1... | collective-permute-start | bytes 1572872 | tf_op jit(solution)/shard_map/ppermute | solution.py:217
  77.6 31.6 %collective-permute-start = (f32[512,128]{1,0:T(8,128)S(1)}, f32[512,128]{1,0:T(8,128)S(1)}, u32[]{:S(2)}, u32[]{:S(2)}) collective-permute-start(f32[512,128]{1,0:T(8,128)S(1)} %copy-done), channel_id=1, source_target_pairs={{0,1},{1,2},{2,3},{3,0},{4,5},{5,6},{6,7},{7,4},{8,9},{9,10},{10,1... | collective-permute-start | bytes 786440 | tf_op jit(solution)/shard_map/ppermute | solution.py:221
  80.0 29.2 %collective-permute-start.1 = (f32[512,128]{1,0:T(8,128)S(1)}, f32[512,128]{1,0:T(8,128)S(1)}, u32[]{:S(2)}, u32[]{:S(2)}) collective-permute-start(f32[512,128]{1,0:T(8,128)S(1)} %copy-done), channel_id=1, source_target_pairs={{0,2},{1,3},{2,0},{3,1},{4,6},{5,7},{6,4},{7,5},{8,10},{9,11},{10,... | collective-permute-start | bytes 786440 | tf_op jit(solution)/shard_map/ppermute | solution.py:221
  83.5 25.8 %collective-permute-start.2 = (f32[512,128]{1,0:T(8,128)S(1)}, f32[512,128]{1,0:T(8,128)S(1)}, u32[]{:S(2)}, u32[]{:S(2)}) collective-permute-start(f32[512,128]{1,0:T(8,128)S(1)} %copy-done), channel_id=1, source_target_pairs={{0,3},{1,0},{2,1},{3,2},{4,7},{5,4},{6,5},{7,6},{8,11},{9,8},{10,9... | collective-permute-start | bytes 786440 | tf_op jit(solution)/shard_map/ppermute | solution.py:221
  90.9 23.3 %collective-permute-start.4 = (f32[64,2,8,128]{3,2,1,0:T(8,128)S(1)}, f32[64,2,8,128]{3,2,1,0:T(8,128)S(1)}, u32[]{:S(2)}, u32[]{:S(2)}) collective-permute-start(f32[64,2,8,128]{3,2,1,0:T(8,128)S(1)} %all-to-all-done.3.mine), channel_id=1, source_target_pairs={{0,4},{4,0},{1,5},{5,1},{2,6},{6,2},{3,7},{7,3},{8,12},{12,8},{9,1... | collective-permute-start | bytes 1572872 | tf_op jit(solution)/shard_map/ppermute | solution.py:235
  109.2 5.0 %copy-start.1 = (f32[512,512]{1,0:T(8,128)S(1)}, f32[512,512]{1,0:T(8,128)}, u32[]{:S(2)}) copy-start(f32[512,512]{1,0:T(8,128)} %slab.1) | copy-start | bytes 3145732

commit v3 on v2

--- a/solution.py
+++ b/solution.py
@@ -35,6 +35,10 @@
     return lax.dot_general(
         a, b, (((1,), (1,)), ((), ())), precision=lax.Precision.HIGHEST, preferred_element_type=F32
     )
+
+
+def mul(a, b):
+    return jnp.dot(a, b, precision=lax.Precision.HIGHEST, preferred_element_type=F32)
 
 
 def mul_t3(a, b):
@@ -100,12 +104,13 @@
 
 
 def unpack(core, mine, other, out):
-    size = out.shape[1]
+    size = out.shape[0]
 
     def place(low, high):
         for half, ref in ((0, low), (1, high)):
             for j in range(2):
-                out[2 * half + j] = ref[:, j].reshape(size, BLOCK)
+                o = (2 * half + j) * BLOCK
+                out[:, o : o + BLOCK] = ref[:, j].reshape(size, BLOCK)
 
     @pl.when(core == 0)
     def _():
@@ -116,67 +121,67 @@
         place(other, mine)
 
 
-def place_of(row_block, col_block):
-    return row_block * (row_block - 1) // 2 + col_block
-
-
-def factor_kernel(idx, mine, other, inverse, lower, a, d):
-    blocks = a.shape[0]
+def factor_kernel(idx, mine, other, top, bottom, a, inverse, d):
+    size = a.shape[0]
+    half = size // 2
     unpack(idx[0], mine, other, a)
     tri = lax.broadcasted_iota(jnp.int32, (BLOCK, BLOCK), 0) >= lax.broadcasted_iota(
         jnp.int32, (BLOCK, BLOCK), 1
     )
-    for j in range(blocks):
-        o = j * BLOCK
+    for o in range(0, size, BLOCK):
         n = o + BLOCK
 
-        def load(t, j=j, o=o):
-            return a[j, o + t * STRIP : o + (t + 1) * STRIP, :]
+        def load(t, o=o, n=n):
+            return a[o + t * STRIP : o + (t + 1) * STRIP, o:n]
 
         def store(t, value):
             d[t * STRIP : (t + 1) * STRIP, :] = value
 
         factor_block(load, store)
         inv = jnp.where(tri, d[...], 0.0)
-        inverse[j] = inv
-        if j + 1 < blocks:
-            below = mul_t(a[j, n:, :], inv)
-            for m in range(j + 1, blocks):
-                lo = (m - j - 1) * BLOCK
-                s = m * BLOCK
-                lower[place_of(m, j)] = below[lo : lo + BLOCK]
-                a[m, s:, :] = a[m, s:, :] - mul_t(below[lo:], below[lo : lo + BLOCK])
-
-
-def solve(x, inverse, lower):
-    blocks = x.shape[0]
-    for j in range(blocks):
-        solved = mul_t(x[j], inverse[j])
-        x[j] = solved
-        for m in range(j + 1, blocks):
-            x[m] = x[m] - mul_t(solved, lower[place_of(m, j)])
-
-
-def own_kernel(idx, own0, own1, own2, own3, inverse, lower, out, factor):
+        inverse[o:n, o:n] = inv
+        if n < size:
+            inverse[o:n, n:] = jnp.zeros((BLOCK, size - n), F32)
+            below = mul_t(a[n:, o:n], inv)
+            a[n:, o:n] = below
+            for m in range(n, size, BLOCK):
+                lo = m - n
+                e = m + BLOCK
+                a[m:, m:e] = a[m:, m:e] - mul_t(below[lo:], below[lo : lo + BLOCK])
+        if o > 0:
+            inverse[o:n, :o] = 0.0 - mul(inv, mul(a[o:n, :o], inverse[:o, :o]))
+    top[...] = inverse[:half, :half]
+    bottom[...] = inverse[half:, :]
+
+
+def solve(x, top, bottom):
+    half = x.shape[1] // 2
+    return mul_t(x[:, :half], top[...]), mul_t(x[...], bottom[...])
+
+
+def own_kernel(idx, own0, own1, own2, own3, top, bottom, out, factor, x):
     col, row_start = idx[1], idx[2]
-    blocks, size = out.shape[0], out.shape[1]
+    size = x.shape[0]
+    half = size // 2
+
+    def lanes_of(block):
+        return pl.ds(pl.multiple_of(block * BLOCK, BLOCK), BLOCK)
+
     for shift, ref in enumerate((own0, own1, own2, own3)):
-        out[lax.rem(col - shift + blocks, blocks)] = ref[...]
-    solve(out, inverse, lower)
-    rows = row_start + lax.broadcasted_iota(jnp.int32, (size, BLOCK), 0)
-    lanes = lax.broadcasted_iota(jnp.int32, (size, BLOCK), 1)
-    for j in range(blocks):
-        out[j] = jnp.where(lanes + j * BLOCK <= rows, out[j], 0.0)
-    factor[...] = out[col]
-
-
-def schur_kernel(idx, own, mine, other, inverse, lower, slab, schur, far):
+        x[:, lanes_of(lax.rem(col - shift + 4, 4))] = ref[...]
+    rows = row_start + lax.broadcasted_iota(jnp.int32, (size, half), 0)
+    lanes = lax.broadcasted_iota(jnp.int32, (size, half), 1)
+    for part, solved in enumerate(solve(x, top, bottom)):
+        o = part * half
+        out[:, o : o + half] = jnp.where(lanes + o <= rows, solved, 0.0)
+    factor[...] = out[:, lanes_of(col)]
+
+
+def schur_kernel(idx, own, mine, other, top, bottom, slab, schur, far):
+    half = far.shape[0] // 2
     unpack(idx[0], mine, other, far)
-    solve(far, inverse, lower)
-    total = slab[...]
-    for j in range(far.shape[0]):
-        total = total - mul_t3(own[j], far[j])
-    schur[...] = total
+    low, high = solve(far, top, bottom)
+    schur[...] = slab[...] - (mul_t3(own[:, :half], low) + mul_t3(own[:, half:], high))
 
 
 def call(body, outs, flops, scratch, *args):
@@ -219,15 +224,15 @@
     own = [kernel_panel]
     for shift in (1, 2, 3):
         own.append(lax.ppermute(kernel_panel, "x", [(i, (i + shift) % 4) for i in range(4)]))
-    blocks = jax.ShapeDtypeStruct((4, size, BLOCK), F32)
-    inverse, lower = call(
+    square = jax.ShapeDtypeStruct((size, size), F32)
+    inverse = call(
         factor_kernel,
         (
-            jax.ShapeDtypeStruct((4, BLOCK, BLOCK), F32),
-            jax.ShapeDtypeStruct((6, BLOCK, BLOCK), F32),
+            jax.ShapeDtypeStruct((size // 2, size // 2), F32),
+            jax.ShapeDtypeStruct((size // 2, size), F32),
         ),
         2 * 10**10,
-        [(4, size, BLOCK), (BLOCK, BLOCK)],
+        [(size, size), (size, size), (BLOCK, BLOCK)],
         idx,
         lead,
         lead_other,
@@ -235,25 +240,23 @@
     far_other = lax.ppermute(far, "k", [(0, 1), (1, 0)])
     own, factor = call(
         own_kernel,
-        (blocks, jax.ShapeDtypeStruct((size, BLOCK), F32)),
+        (square, jax.ShapeDtypeStruct((size, BLOCK), F32)),
         2 * 10**9,
-        [],
+        [(size, size)],
         idx,
         *own,
-        inverse,
-        lower,
+        *inverse,
     )
     (schur,) = call(
         schur_kernel,
-        (jax.ShapeDtypeStruct((size, size), F32),),
+        (square,),
         4 * 10**9,
-        [(4, size, BLOCK)],
+        [(size, size)],
         idx,
         own,
         far,
         far_other,
-        inverse,
-        lower,
+        *inverse,
         kernel_slab,
     )
     return factor, schur

time: 122 us -> 118 us (0.967)
  Pallas kernels: 24.2 us -> 21 us
    pallas_call x3, Pallas kernels: 24.2 us -> 21 us  [call(): pl.pallas_call(body, out_shape=outs, in_specs=[pl.BlockSpec(memory_space=...]
where the time goes in v3:
time: 118 us
  starting transfers between devices  36.3 us (31%)
  blocking collectives  30 us (25%)
  waiting for transfers between devices  27.3 us (23%)
  Pallas kernels  21 us (18%)
  local copies, waits for them, and re-layouts  2.33 us (2%)
    all_to_all x1, blocking collectives, plan(): lax.all_to_all(kernel_panel.reshape(64, 8, BLOCK), PLANE, 0, 0, tiled=True)  30 us
    all_to_all x2, waiting for transfers between devices, spread(): return lax.all_to_all(copies, PLANE, 0, 0, tiled=True)  22.3 us
    pallas_call x3, Pallas kernels, call(): pl.pallas_call(body, out_shape=outs, in_specs=[pl.BlockSpec(memory_space=...  21 us
    all_to_all x2, starting transfers between devices, spread(): return lax.all_to_all(copies, PLANE, 0, 0, tiled=True)  11.1 us
    ppermute x3, starting transfers between devices, plan(): lax.ppermute(kernel_panel, 'x', [(i, (i + shift) % 4) for i in range(4)])  8.68 us
    all_to_all x1, starting transfers between devices, plan(): lax.all_to_all(parcel, ('k', 'x'), 0, 0, tiled=True)  7.36 us
    ppermute x1, starting transfers between devices, plan(): far_other = lax.ppermute(far, 'k', [(0, 1), (1, 0)])  5.8 us
    all_to_all x1, waiting for transfers between devices, plan(): lax.all_to_all(parcel, ('k', 'x'), 0, 0, tiled=True)  4.97 us
  transfers between devices with their start and end apart: 8, of which 3 were waited for; matrix products, arithmetic and copies ran while one was open for 0% of the time, Pallas kernels for 14%

profile of v3, /device:TPU:1, one launch (start us, length us, event | category | flops | bytes accessed | tf_op | source)
XLA Modules:
  0.0 117.8 jit_solution(2685683132429226796)
XLA Ops:
  0.6 30.0 %all_to_all.20 = f32[64,8,128]{2,1,0:T(8,128)S(1)} all-to-all(f32[64,8,128]{2,1,0:T(8,128)} %bitcast.16), channel_id=1, replica_groups=mesh['z'=8,'y'=8,'k'=2,'x'=4] {'z','y'}, dimensions={0} | all-to-all | bytes 524288 | tf_op jit(solution)/shard_map/all_to_all | solution.py:209
  30.6 0.6 broadcast_in_dim.10
  31.3 7.4 %all-to-all-start.1 = ((f32[8,2,8,128]{3,2,1,0:T(8,128)}), f32[8,2,8,128]{3,2,1,0:T(8,128)S(1)}, u32[]{:S(2)}, u32[]{:S(2)}) async-start(f32[8,2,8,128]{3,2,1,0:T(8,128)} %bitcast.7), calls=%async_computation.1 | async-start | bytes 131072 | tf_op jit(solution)/shard_map/all_to_all | solution.py:212
  38.6 5.0 %all-to-all-done.1 = f32[8,2,8,128]{3,2,1,0:T(8,128)S(1)} async-done(((f32[8,2,8,128]{3,2,1,0:T(8,128)}), f32[8,2,8,128]{3,2,1,0:T(8,128)S(1)}, u32[]{:S(2)}, u32[]{:S(2)}) %all-to-all-start.1) | async-done | bytes 65568 | tf_op jit(solution)/shard_map/all_to_all | solution.py:212
  43.6 0.8 broadcast_in_dim.24
  44.4 4.6 %all-to-all-start.2 = ((f32[64,2,8,128]{3,2,1,0:T(8,128)}), f32[64,2,8,128]{3,2,1,0:T(8,128)S(1)}, u32[]{:S(2)}, u32[]{:S(2)}) async-start(f32[64,2,8,128]{3,2,1,0:T(8,128)} %broadcast_in_dim.24), calls=%async_computation.2 | async-start | bytes 1048576 | tf_op jit(solution)/shard_map/all_to_all | solution.py:219
  49.1 17.8 %all-to-all-done.2.mine = f32[64,2,8,128]{3,2,1,0:T(8,128)S(1)} async-done(((f32[64,2,8,128]{3,2,1,0:T(8,128)}), f32[64,2,8,128]{3,2,1,0:T(8,128)S(1)}, u32[]{:S(2)}, u32[]{:S(2)}) %all-to-all-start.2) | async-done | bytes 524320 | tf_op jit(solution)/shard_map/all_to_all | solution.py:219
  67.0 0.8 broadcast_in_dim.26
  67.8 6.5 %all-to-all-start.3 = ((f32[64,2,8,128]{3,2,1,0:T(8,128)}), f32[64,2,8,128]{3,2,1,0:T(8,128)S(1)}, u32[]{:S(2)}, u32[]{:S(2)}) async-start(f32[64,2,8,128]{3,2,1,0:T(8,128)} %broadcast_in_dim.26), calls=%async_computation.3 | async-start | bytes 1048576 | tf_op jit(solution)/shard_map/all_to_all | solution.py:219
  74.3 3.3 %collective-permute-start.3 = (f32[64,2,8,128]{3,2,1,0:T(8,128)S(1)}, f32[64,2,8,128]{3,2,1,0:T(8,128)S(1)}, u32[]{:S(2)}, u32[]{:S(2)}) collective-permute-start(f32[64,2,8,128]{3,2,1,0:T(8,128)S(1)} %all-to-all-done.2.mine), channel_id=1, source_target_pairs={{0,4},{4,0},{1,5},{5,1},{2,6},{6,2},{3,7},{7,3},{8,12},{12,8},{9,1... | collective-permute-start | bytes 1572872 | tf_op jit(solution)/shard_map/ppermute | solution.py:222
  77.6 2.4 %collective-permute-start = (f32[512,128]{1,0:T(8,128)S(1)}, f32[512,128]{1,0:T(8,128)S(1)}, u32[]{:S(2)}, u32[]{:S(2)}) collective-permute-start(f32[512,128]{1,0:T(8,128)S(1)} %copy-done), channel_id=1, source_target_pairs={{0,1},{1,2},{2,3},{3,0},{4,5},{5,6},{6,7},{7,4},{8,9},{9,10},{10,1... | collective-permute-start | bytes 786440 | tf_op jit(solution)/shard_map/ppermute | solution.py:226
  80.0 3.4 %collective-permute-start.1 = (f32[512,128]{1,0:T(8,128)S(1)}, f32[512,128]{1,0:T(8,128)S(1)}, u32[]{:S(2)}, u32[]{:S(2)}) collective-permute-start(f32[512,128]{1,0:T(8,128)S(1)} %copy-done), channel_id=1, source_target_pairs={{0,2},{1,3},{2,0},{3,1},{4,6},{5,7},{6,4},{7,5},{8,10},{9,11},{10,... | collective-permute-start | bytes 786440 | tf_op jit(solution)/shard_map/ppermute | solution.py:226
  83.5 2.9 %collective-permute-start.2 = (f32[512,128]{1,0:T(8,128)S(1)}, f32[512,128]{1,0:T(8,128)S(1)}, u32[]{:S(2)}, u32[]{:S(2)}) collective-permute-start(f32[512,128]{1,0:T(8,128)S(1)} %copy-done), channel_id=1, source_target_pairs={{0,3},{1,0},{2,1},{3,2},{4,7},{5,4},{6,5},{7,6},{8,11},{9,8},{10,9... | collective-permute-start | bytes 786440 | tf_op jit(solution)/shard_map/ppermute | solution.py:226
  86.3 0.1 pad_add_fusion.idx
  86.4 4.5 %all-to-all-done.3.mine = f32[64,2,8,128]{3,2,1,0:T(8,128)S(1)} async-done(((f32[64,2,8,128]{3,2,1,0:T(8,128)}), f32[64,2,8,128]{3,2,1,0:T(8,128)S(1)}, u32[]{:S(2)}, u32[]{:S(2)}) %all-to-all-start.3) | async-done | bytes 524320 | tf_op jit(solution)/shard_map/all_to_all | solution.py:219
  90.9 5.8 %collective-permute-start.4 = (f32[64,2,8,128]{3,2,1,0:T(8,128)S(1)}, f32[64,2,8,128]{3,2,1,0:T(8,128)S(1)}, u32[]{:S(2)}, u32[]{:S(2)}) collective-permute-start(f32[64,2,8,128]{3,2,1,0:T(8,128)S(1)} %all-to-all-done.3.mine), channel_id=1, source_target_pairs={{0,4},{4,0},{1,5},{5,1},{2,6},{6,2},{3,7},{7,3},{8,12},{12,8},{9,1... | collective-permute-start | bytes 1572872 | tf_op jit(solution)/shard_map/ppermute | solution.py:240
  96.7 0.0 collective-permute-done.3.other
  96.8 13.0 %shard_map.41 = (f32[256,256]{1,0:T(8,128)S(1)}, f32[256,512]{1,0:T(8,128)S(1)}) custom-call(s32[3]{0:T(128)S(1)} %pad_add_fusion.idx, f32[64,2,8,128]{3,2,1,0:T(8,128)S(1)} %all-to-all-done.2.mine, f32[64,2,8,128]{3,2,1,0:T(8,128)S(1)} %collective-permute-done.3.other), custom_call_target="tpu_custom_call" | custom-call | flops 20000000000 | bytes 1835020 | tf_op jit(solution)/shard_map/pallas_call | solution.py:190
  109.8 0.0 collective-permute-done.own1
  109.8 0.0 collective-permute-done.1.own2
  109.8 0.0 collective-permute-done.2.own3
  109.8 0.0 copy-start.1
  109.8 3.2 %shard_map.42 = (f32[512,512]{1,0:T(8,128)S(1)}, f32[512,128]{1,0:T(8,128)}) custom-call(s32[3]{0:T(128)S(1)} %pad_add_fusion.idx, f32[512,128]{1,0:T(8,128)S(1)} %copy-done, f32[512,128]{1,0:T(8,128)S(1)} %collective-permute-done.own1, f32[512,128]{1,0:T(8,128)S(1)} %collective-permute-done.1.own2, f32[512,128]{1,0:T(8,128)S(1)} %collective-permute-done.2.own3, ...), custom_call_target="tpu_custom_call" | custom-call | flops 2000000000 | bytes 3145740 | tf_op jit(solution)/shard_map/pallas_call | solution.py:190
  113.0 4.8 %shard_map.43 = f32[512,512]{1,0:T(8,128)} custom-call(s32[3]{0:T(128)S(1)} %pad_add_fusion.idx, f32[512,512]{1,0:T(8,128)S(1)} %get-tuple-element.9.own, f32[64,2,8,128]{3,2,1,0:T(8,128)S(1)} %all-to-all-done.3.mine, f32[64,2,8,128]{3,2,1,0:T(8,128)S(1)} %collective-permute-done.4.other, f32[256,256]{1,0:T(8,128)S(1)} %get-tuple-element.6.top, ...), custom_call_target="tpu_custom_call" | custom-call | flops 4000000000 | bytes 4980748 | tf_op jit(solution)/shard_map/pallas_call | solution.py:190
  (11 shorter events, 0.0 us)
Async XLA Ops:
  31.3 12.3 %all-to-all-start.1 = ((f32[8,2,8,128]{3,2,1,0:T(8,128)}), f32[8,2,8,128]{3,2,1,0:T(8,128)S(1)}, u32[]{:S(2)}, u32[]{:S(2)}) async-start(f32[8,2,8,128]{3,2,1,0:T(8,128)} %bitcast.7), calls=%async_computation.1 | async-start | bytes 131072 | tf_op jit(solution)/shard_map/all_to_all | solution.py:212
  44.4 22.5 %all-to-all-start.2 = ((f32[64,2,8,128]{3,2,1,0:T(8,128)}), f32[64,2,8,128]{3,2,1,0:T(8,128)S(1)}, u32[]{:S(2)}, u32[]{:S(2)}) async-start(f32[64,2,8,128]{3,2,1,0:T(8,128)} %broadcast_in_dim.24), calls=%async_computation.2 | async-start | bytes 1048576 | tf_op jit(solution)/shard_map/all_to_all | solution.py:219
  67.8 9.8 %copy-start = (f32[512,128]{1,0:T(8,128)S(1)}, f32[512,128]{1,0:T(8,128)}, u32[]{:S(2)}) copy-start(f32[512,128]{1,0:T(8,128)} %own0.1) | copy-start | bytes 786436
  67.8 23.1 %all-to-all-start.3 = ((f32[64,2,8,128]{3,2,1,0:T(8,128)}), f32[64,2,8,128]{3,2,1,0:T(8,128)S(1)}, u32[]{:S(2)}, u32[]{:S(2)}) async-start(f32[64,2,8,128]{3,2,1,0:T(8,128)} %broadcast_in_dim.26), calls=%async_computation.3 | async-start | bytes 1048576 | tf_op jit(solution)/shard_map/all_to_all | solution.py:219
  74.3 22.5 %collective-permute-start.3 = (f32[64,2,8,128]{3,2,1,0:T(8,128)S(1)}, f32[64,2,8,128]{3,2,1,0:T(8,128)S(1)}, u32[]{:S(2)}, u32[]{:S(2)}) collective-permute-start(f32[64,2,8,128]{3,2,1,0:T(8,128)S(1)} %all-to-all-done.2.mine), channel_id=1, source_target_pairs={{0,4},{4,0},{1,5},{5,1},{2,6},{6,2},{3,7},{7,3},{8,12},{12,8},{9,1... | collective-permute-start | bytes 1572872 | tf_op jit(solution)/shard_map/ppermute | solution.py:222
  77.6 32.2 %collective-permute-start = (f32[512,128]{1,0:T(8,128)S(1)}, f32[512,128]{1,0:T(8,128)S(1)}, u32[]{:S(2)}, u32[]{:S(2)}) collective-permute-start(f32[512,128]{1,0:T(8,128)S(1)} %copy-done), channel_id=1, source_target_pairs={{0,1},{1,2},{2,3},{3,0},{4,5},{5,6},{6,7},{7,4},{8,9},{9,10},{10,1... | collective-permute-start | bytes 786440 | tf_op jit(solution)/shard_map/ppermute | solution.py:226
  80.0 29.8 %collective-permute-start.1 = (f32[512,128]{1,0:T(8,128)S(1)}, f32[512,128]{1,0:T(8,128)S(1)}, u32[]{:S(2)}, u32[]{:S(2)}) collective-permute-start(f32[512,128]{1,0:T(8,128)S(1)} %copy-done), channel_id=1, source_target_pairs={{0,2},{1,3},{2,0},{3,1},{4,6},{5,7},{6,4},{7,5},{8,10},{9,11},{10,... | collective-permute-start | bytes 786440 | tf_op jit(solution)/shard_map/ppermute | solution.py:226
  83.5 26.3 %collective-permute-start.2 = (f32[512,128]{1,0:T(8,128)S(1)}, f32[512,128]{1,0:T(8,128)S(1)}, u32[]{:S(2)}, u32[]{:S(2)}) collective-permute-start(f32[512,128]{1,0:T(8,128)S(1)} %copy-done), channel_id=1, source_target_pairs={{0,3},{1,0},{2,1},{3,2},{4,7},{5,4},{6,5},{7,6},{8,11},{9,8},{10,9... | collective-permute-start | bytes 786440 | tf_op jit(solution)/shard_map/ppermute | solution.py:226
  90.9 22.1 %collective-permute-start.4 = (f32[64,2,8,128]{3,2,1,0:T(8,128)S(1)}, f32[64,2,8,128]{3,2,1,0:T(8,128)S(1)}, u32[]{:S(2)}, u32[]{:S(2)}) collective-permute-start(f32[64,2,8,128]{3,2,1,0:T(8,128)S(1)} %all-to-all-done.3.mine), channel_id=1, source_target_pairs={{0,4},{4,0},{1,5},{5,1},{2,6},{6,2},{3,7},{7,3},{8,12},{12,8},{9,1... | collective-permute-start | bytes 1572872 | tf_op jit(solution)/shard_map/ppermute | solution.py:240
  109.8 3.2 %copy-start.1 = (f32[512,512]{1,0:T(8,128)S(1)}, f32[512,512]{1,0:T(8,128)}, u32[]{:S(2)}) copy-start(f32[512,512]{1,0:T(8,128)} %slab.1) | copy-start | bytes 3145732

commit v4 on v3

--- a/solution.py
+++ b/solution.py
@@ -14,6 +14,7 @@
 BLOCK = 128
 STRIPS = BLOCK // STRIP
 AHEAD = 3
+CHUNKS = 4
 
 
 def split3(x):
@@ -59,12 +60,16 @@
     return jnp.broadcast_to(x[r : r + 1, :], (STRIP, BLOCK))
 
 
-def factor_block(load, store):
+def factor_block(load, store, background=()):
+    background = list(background)
+    every = -(-STRIPS // max(len(background), 1))
     row = lax.broadcasted_iota(jnp.int32, (STRIP, BLOCK), 0)
     lane = lax.broadcasted_iota(jnp.int32, (STRIP, BLOCK), 1)
     rows = [load(t) for t in range(STRIPS)]
     spread = {}
     for b in range(STRIPS):
+        if background and b % every == 0:
+            background.pop(0)()
         o = b * STRIP
         window = range(b, min(b + AHEAD + 1, STRIPS))
         below = window[1:]
@@ -103,14 +108,14 @@
                 rows[t] = jnp.where(inside, 0.0, rows[t]) - update[t * STRIP : (t + 1) * STRIP]
 
 
-def unpack(core, mine, other, out):
-    size = out.shape[0]
+def unpack(core, mine, other, item, out, start):
+    size = mine.shape[0] * mine.shape[2]
 
     def place(low, high):
         for half, ref in ((0, low), (1, high)):
             for j in range(2):
                 o = (2 * half + j) * BLOCK
-                out[:, o : o + BLOCK] = ref[:, j].reshape(size, BLOCK)
+                out[start : start + size, o : o + BLOCK] = ref[:, item + j].reshape(size, BLOCK)
 
     @pl.when(core == 0)
     def _():
@@ -121,13 +126,30 @@
         place(other, mine)
 
 
-def factor_kernel(idx, mine, other, top, bottom, a, inverse, d):
+def kernel(idx, mine, other, own0, own1, own2, own3, slab, factor, schur, a, inverse, d, x, f):
+    core, col, row_start = idx[0], idx[1], idx[2]
     size = a.shape[0]
     half = size // 2
-    unpack(idx[0], mine, other, a)
+    unpack(core, mine, other, 0, a, 0)
+    unpack(core, mine, other, 2, x, size)
+
+    def lanes_of(block):
+        return pl.ds(pl.multiple_of(block * BLOCK, BLOCK), BLOCK)
+
+    for shift, ref in enumerate((own0, own1, own2, own3)):
+        x[:size, lanes_of(lax.rem(col - shift + 4, 4))] = ref[...]
     tri = lax.broadcasted_iota(jnp.int32, (BLOCK, BLOCK), 0) >= lax.broadcasted_iota(
         jnp.int32, (BLOCK, BLOCK), 1
     )
+
+    def solve(first, last, chunks):
+        rows = 2 * size // chunks
+
+        def chunk(r):
+            f[r : r + rows, first:last] = mul_t(x[r : r + rows, :last], inverse[first:last, :last])
+
+        return [lambda r=r: chunk(r) for r in range(0, 2 * size, rows)]
+
     for o in range(0, size, BLOCK):
         n = o + BLOCK
 
@@ -137,7 +159,13 @@
         def store(t, value):
             d[t * STRIP : (t + 1) * STRIP, :] = value
 
-        factor_block(load, store)
+        if o == half:
+            background = solve(0, half, CHUNKS)
+        elif o == half + BLOCK:
+            background = solve(half, o, CHUNKS)
+        else:
+            background = ()
+        factor_block(load, store, background)
         inv = jnp.where(tri, d[...], 0.0)
         inverse[o:n, o:n] = inv
         if n < size:
@@ -150,54 +178,35 @@
                 a[m:, m:e] = a[m:, m:e] - mul_t(below[lo:], below[lo : lo + BLOCK])
         if o > 0:
             inverse[o:n, :o] = 0.0 - mul(inv, mul(a[o:n, :o], inverse[:o, :o]))
-    top[...] = inverse[:half, :half]
-    bottom[...] = inverse[half:, :]
-
-
-def solve(x, top, bottom):
-    half = x.shape[1] // 2
-    return mul_t(x[:, :half], top[...]), mul_t(x[...], bottom[...])
-
-
-def own_kernel(idx, own0, own1, own2, own3, top, bottom, out, factor, x):
-    col, row_start = idx[1], idx[2]
-    size = x.shape[0]
-    half = size // 2
-
-    def lanes_of(block):
-        return pl.ds(pl.multiple_of(block * BLOCK, BLOCK), BLOCK)
-
-    for shift, ref in enumerate((own0, own1, own2, own3)):
-        x[:, lanes_of(lax.rem(col - shift + 4, 4))] = ref[...]
-    rows = row_start + lax.broadcasted_iota(jnp.int32, (size, half), 0)
-    lanes = lax.broadcasted_iota(jnp.int32, (size, half), 1)
-    for part, solved in enumerate(solve(x, top, bottom)):
-        o = part * half
-        out[:, o : o + half] = jnp.where(lanes + o <= rows, solved, 0.0)
-    factor[...] = out[:, lanes_of(col)]
-
-
-def schur_kernel(idx, own, mine, other, top, bottom, slab, schur, far):
-    half = far.shape[0] // 2
-    unpack(idx[0], mine, other, far)
-    low, high = solve(far, top, bottom)
-    schur[...] = slab[...] - (mul_t3(own[:, :half], low) + mul_t3(own[:, half:], high))
-
-
-def call(body, outs, flops, scratch, *args):
+    solve(size - BLOCK, size, 1)[0]()
+    rows = row_start + lax.broadcasted_iota(jnp.int32, (size, size), 0)
+    lanes = lax.broadcasted_iota(jnp.int32, (size, size), 1)
+    f[:size, :] = jnp.where(lanes <= rows, f[:size, :], 0.0)
+    factor[...] = f[:size, lanes_of(col)]
+    schur[...] = slab[...] - mul_t3(f[:size, :], f[size:, :])
+
+
+def run_kernel(idx, mine, other, own0, own1, own2, own3, slab):
+    size = slab.shape[0]
     vmem = pl.BlockSpec(memory_space=pltpu.VMEM)
-    bytes_accessed = sum(4 * a.size for a in args) + sum(4 * o.size for o in outs)
     return pl.pallas_call(
-        body,
-        out_shape=outs,
-        in_specs=[pl.BlockSpec(memory_space=pltpu.SMEM)] + [vmem] * (len(args) - 1),
-        out_specs=tuple(vmem for _ in outs),
-        scratch_shapes=[pltpu.VMEM(s, F32) for s in scratch],
+        kernel,
+        name="factor",
+        out_shape=(
+            jax.ShapeDtypeStruct((size, BLOCK), F32),
+            jax.ShapeDtypeStruct((size, size), F32),
+        ),
+        in_specs=[pl.BlockSpec(memory_space=pltpu.SMEM)] + [vmem] * 7,
+        out_specs=(vmem, vmem),
+        scratch_shapes=[
+            pltpu.VMEM((size, size), F32),
+            pltpu.VMEM((size, size), F32),
+            pltpu.VMEM((BLOCK, BLOCK), F32),
+            pltpu.VMEM((2 * size, size), F32),
+            pltpu.VMEM((2 * size, size), F32),
+        ],
         compiler_params=pltpu.CompilerParams(vmem_limit_bytes=16 << 20),
-        cost_estimate=pl.CostEstimate(
-            flops=flops, bytes_accessed=bytes_accessed, transcendentals=0
-        ),
-    )(*args)
+    )(idx, mine, other, own0, own1, own2, own3, slab)
 
 
 def plan(kernel_panel, kernel_slab):
@@ -214,52 +223,13 @@
     far = lax.dynamic_index_in_dim(parcel[:, :, 1], lax.rem(1 + col, 2), 0, keepdims=False)
     far = lax.dynamic_slice_in_dim(far, 2 * core, 2, 0)
 
-    def spread(piece):
-        copies = jnp.broadcast_to(piece[None], (64, 2, 8, BLOCK))
-        return lax.all_to_all(copies, PLANE, 0, 0, tiled=True)
-
-    lead = spread(lead)
-    lead_other = lax.ppermute(lead, "k", [(0, 1), (1, 0)])
-    far = spread(far)
+    copies = jnp.broadcast_to(jnp.concatenate([lead, far])[None], (64, 4, 8, BLOCK))
+    mine = lax.all_to_all(copies, PLANE, 0, 0, tiled=True)
+    other = lax.ppermute(mine, "k", [(0, 1), (1, 0)])
     own = [kernel_panel]
     for shift in (1, 2, 3):
         own.append(lax.ppermute(kernel_panel, "x", [(i, (i + shift) % 4) for i in range(4)]))
-    square = jax.ShapeDtypeStruct((size, size), F32)
-    inverse = call(
-        factor_kernel,
-        (
-            jax.ShapeDtypeStruct((size // 2, size // 2), F32),
-            jax.ShapeDtypeStruct((size // 2, size), F32),
-        ),
-        2 * 10**10,
-        [(size, size), (size, size), (BLOCK, BLOCK)],
-        idx,
-        lead,
-        lead_other,
-    )
-    far_other = lax.ppermute(far, "k", [(0, 1), (1, 0)])
-    own, factor = call(
-        own_kernel,
-        (square, jax.ShapeDtypeStruct((size, BLOCK), F32)),
-        2 * 10**9,
-        [(size, size)],
-        idx,
-        *own,
-        *inverse,
-    )
-    (schur,) = call(
-        schur_kernel,
-        (square,),
-        4 * 10**9,
-        [(size, size)],
-        idx,
-        own,
-        far,
-        far_other,
-        *inverse,
-        kernel_slab,
-    )
-    return factor, schur
+    return run_kernel(idx, mine, other, *own, kernel_slab)
 
 
 def solution(mesh):

time: 118 us -> 118 us (level)
  blocking collectives: 30 us -> 62.1 us
  starting transfers between devices: 36.3 us -> 21 us
  waiting for transfers between devices: 27.3 us -> 12.9 us
  local copies, waits for them, and re-layouts: 2.33 us -> 0.78 us
  Pallas kernels: 21 us -> 19.8 us
    all_to_all x0 -> x1, blocking collectives: none -> 32.1 us  [plan(): mine = lax.all_to_all(copies, PLANE, 0, 0, tiled=True)]
    all_to_all x2 -> x0, waiting for transfers between devices: 22.3 us -> none  [spread(): return lax.all_to_all(copies, PLANE, 0, 0, tiled=True)]
    all_to_all x2 -> x0, starting transfers between devices: 11.1 us -> none  [spread(): return lax.all_to_all(copies, PLANE, 0, 0, tiled=True)]
    ppermute x3, waiting for transfers between devices: 0.01 us -> 7.97 us  [plan(): lax.ppermute(kernel_panel, 'x', [(i, (i + shift) % 4) for i in range(4)])]
    ppermute x2 -> x1, starting transfers between devices: 9.12 us -> 4.32 us  [plan(): other = lax.ppermute(mine, 'k', [(0, 1), (1, 0)])]
    broadcast_in_dim x4 -> x1, local copies, waits for them, and re-layouts: 1.67 us -> 0.12 us  [plan(): jnp.broadcast_to(jnp.concatenate([lead, far])[None], (64, 4, 8, BLOCK))]
    pallas_call x3 -> x1, Pallas kernels: 21 us -> 19.8 us  [run_kernel(): pl.pallas_call(kernel, name='factor', out_shape=(jax.ShapeDtypeStruct((si...]
  transfers between devices with their start and end apart: 8 -> 5, of which waited for: 3 -> 3; matrix products, arithmetic and copies ran while one was open for 0% -> 0% of each run, Pallas kernels for 14% -> 0%
where the time goes in v4:
time: 118 us; the launch traced here: 117 us
  blocking collectives  62.1 us (53%)
  starting transfers between devices  21 us (18%)
  Pallas kernels  19.8 us (17%)
  waiting for transfers between devices  12.9 us (11%)
    all_to_all x1, blocking collectives, plan(): mine = lax.all_to_all(copies, PLANE, 0, 0, tiled=True)  32.1 us
    all_to_all x1, blocking collectives, plan(): lax.all_to_all(kernel_panel.reshape(64, 8, BLOCK), PLANE, 0, 0, tiled=True)  30 us
    pallas_call x1, Pallas kernels, run_kernel(): pl.pallas_call(kernel, name='factor', out_shape=(jax.ShapeDtypeStruct((si...  19.8 us
    ppermute x3, starting transfers between devices, plan(): lax.ppermute(kernel_panel, 'x', [(i, (i + shift) % 4) for i in range(4)])  9.29 us
    ppermute x3, waiting for transfers between devices, plan(): lax.ppermute(kernel_panel, 'x', [(i, (i + shift) % 4) for i in range(4)])  7.97 us
    all_to_all x1, starting transfers between devices, plan(): lax.all_to_all(parcel, ('k', 'x'), 0, 0, tiled=True)  7.36 us
    all_to_all x1, waiting for transfers between devices, plan(): lax.all_to_all(parcel, ('k', 'x'), 0, 0, tiled=True)  4.97 us
    ppermute x1, starting transfers between devices, plan(): other = lax.ppermute(mine, 'k', [(0, 1), (1, 0)])  4.32 us
  transfers between devices with their start and end apart: 5, of which 3 were waited for; matrix products, arithmetic and copies ran while one was open for 0% of the time, Pallas kernels for 0%

profile of v4, /device:TPU:1, one launch (start us, length us, event | category | flops | bytes accessed | tf_op | source)
XLA Modules:
  0.0 117.4 jit_solution(11556574575340524799)
XLA Ops:
  0.6 30.0 %all_to_all.15 = f32[64,8,128]{2,1,0:T(8,128)S(1)} all-to-all(f32[64,8,128]{2,1,0:T(8,128)} %bitcast.16), channel_id=1, replica_groups=mesh['z'=8,'y'=8,'k'=2,'x'=4] {'z','y'}, dimensions={0} | all-to-all | bytes 524288 | tf_op jit(solution)/shard_map/all_to_all | solution.py:218
  30.6 0.6 broadcast_in_dim.4
  31.3 7.4 %all-to-all-start.1 = ((f32[8,2,8,128]{3,2,1,0:T(8,128)}), f32[8,2,8,128]{3,2,1,0:T(8,128)S(1)}, u32[]{:S(2)}, u32[]{:S(2)}) async-start(f32[8,2,8,128]{3,2,1,0:T(8,128)} %bitcast.7), calls=%async_computation.1 | async-start | bytes 131072 | tf_op jit(solution)/shard_map/all_to_all | solution.py:221
  38.6 5.0 %all-to-all-done.1 = f32[8,2,8,128]{3,2,1,0:T(8,128)S(1)} async-done(((f32[8,2,8,128]{3,2,1,0:T(8,128)}), f32[8,2,8,128]{3,2,1,0:T(8,128)S(1)}, u32[]{:S(2)}, u32[]{:S(2)}) %all-to-all-start.1) | async-done | bytes 65568 | tf_op jit(solution)/shard_map/all_to_all | solution.py:221
  43.6 0.1 broadcast_in_dim.5
  43.7 0.0 copy-start.1
  43.8 0.0 copy-start
  43.8 32.1 %all_to_all.16.mine = f32[64,4,8,128]{3,2,1,0:T(8,128)S(1)} all-to-all(f32[64,4,8,128]{3,2,1,0:T(8,128)S(1)} %broadcast_in_dim.5), channel_id=1, replica_groups=mesh['z'=8,'y'=8,'k'=2,'x'=4] {'z','y'}, dimensions={0} | all-to-all | bytes 2097152 | tf_op jit(solution)/shard_map/all_to_all | solution.py:227
  75.9 4.3 %collective-permute-start = (f32[64,4,8,128]{3,2,1,0:T(8,128)S(1)}, f32[64,4,8,128]{3,2,1,0:T(8,128)S(1)}, u32[]{:S(2)}, u32[]{:S(2)}) collective-permute-start(f32[64,4,8,128]{3,2,1,0:T(8,128)S(1)} %all_to_all.16.mine), channel_id=1, source_target_pairs={{0,4},{4,0},{1,5},{5,1},{2,6},{6,2},{3,7},{7,3},{8,12},{12,8},{9,1... | collective-permute-start | bytes 3145736 | tf_op jit(solution)/shard_map/ppermute | solution.py:228
  80.2 0.0 copy-done.1
  80.2 2.8 %collective-permute-start.2 = (f32[512,128]{1,0:T(8,128)S(1)}, f32[512,128]{1,0:T(8,128)}, u32[]{:S(2)}, u32[]{:S(2)}) collective-permute-start(f32[512,128]{1,0:T(8,128)S(1)} %copy-done.1), channel_id=1, source_target_pairs={{0,2},{1,3},{2,0},{3,1},{4,6},{5,7},{6,4},{7,5},{8,10},{9,11},{10,... | collective-permute-start | bytes 786440 | tf_op jit(solution)/shard_map/ppermute | solution.py:231
  83.0 2.5 %collective-permute-start.1 = (f32[512,128]{1,0:T(8,128)S(1)}, f32[512,128]{1,0:T(8,128)}, u32[]{:S(2)}, u32[]{:S(2)}) collective-permute-start(f32[512,128]{1,0:T(8,128)S(1)} %copy-done.1), channel_id=1, source_target_pairs={{0,1},{1,2},{2,3},{3,0},{4,5},{5,6},{6,7},{7,4},{8,9},{9,10},{10,1... | collective-permute-start | bytes 786440 | tf_op jit(solution)/shard_map/ppermute | solution.py:231
  85.5 4.0 %collective-permute-start.3 = (f32[512,128]{1,0:T(8,128)S(1)}, f32[512,128]{1,0:T(8,128)}, u32[]{:S(2)}, u32[]{:S(2)}) collective-permute-start(f32[512,128]{1,0:T(8,128)S(1)} %copy-done.1), channel_id=1, source_target_pairs={{0,3},{1,0},{2,1},{3,2},{4,7},{5,4},{6,5},{7,6},{8,11},{9,8},{10,9... | collective-permute-start | bytes 786440 | tf_op jit(solution)/shard_map/ppermute | solution.py:231
  89.5 0.1 pad_add_fusion.idx
  89.6 2.0 %collective-permute-done.2.own2 = f32[512,128]{1,0:T(8,128)} collective-permute-done((f32[512,128]{1,0:T(8,128)S(1)}, f32[512,128]{1,0:T(8,128)}, u32[]{:S(2)}, u32[]{:S(2)}) %collective-permute-start.2) | collective-permute-done | bytes 262176 | tf_op jit(solution)/shard_map/ppermute | solution.py:231
  91.6 6.0 %collective-permute-done.1.own1 = f32[512,128]{1,0:T(8,128)} collective-permute-done((f32[512,128]{1,0:T(8,128)S(1)}, f32[512,128]{1,0:T(8,128)}, u32[]{:S(2)}, u32[]{:S(2)}) %collective-permute-start.1) | collective-permute-done | bytes 262176 | tf_op jit(solution)/shard_map/ppermute | solution.py:231
  97.6 0.0 collective-permute-done.3.own3
  97.6 0.0 collective-permute-done.other
  97.6 0.0 copy-done
  97.6 19.8 %factor.1 = (f32[512,128]{1,0:T(8,128)}, f32[512,512]{1,0:T(8,128)}) custom-call(s32[3]{0:T(128)S(1)} %pad_add_fusion.idx, f32[64,4,8,128]{3,2,1,0:T(8,128)S(1)} %all_to_all.16.mine, f32[64,4,8,128]{3,2,1,0:T(8,128)S(1)} %collective-permute-done.other, f32[512,128]{1,0:T(8,128)S(1)} %copy-done.1, f32[512,128]{1,0:T(8,128)} %collective-permute-done.1.own1, ...), custom_call_target="tpu_custom_call" | custom-call | tf_op jit(solution)/shard_map/factor/pallas_call | solution.py:192
  (8 shorter events, 0.0 us)
Async XLA Ops:
  31.3 12.3 %all-to-all-start.1 = ((f32[8,2,8,128]{3,2,1,0:T(8,128)}), f32[8,2,8,128]{3,2,1,0:T(8,128)S(1)}, u32[]{:S(2)}, u32[]{:S(2)}) async-start(f32[8,2,8,128]{3,2,1,0:T(8,128)} %bitcast.7), calls=%async_computation.1 | async-start | bytes 131072 | tf_op jit(solution)/shard_map/all_to_all | solution.py:221
  43.7 36.5 %copy-start.1 = (f32[512,128]{1,0:T(8,128)S(1)}, f32[512,128]{1,0:T(8,128)}, u32[]{:S(2)}) copy-start(f32[512,128]{1,0:T(8,128)} %own0.1) | copy-start | bytes 786436
  43.8 53.8 %copy-start = (f32[512,512]{1,0:T(8,128)S(1)}, f32[512,512]{1,0:T(8,128)}, u32[]{:S(2)}) copy-start(f32[512,512]{1,0:T(8,128)} %slab.1) | copy-start | bytes 3145732
  75.9 21.7 %collective-permute-start = (f32[64,4,8,128]{3,2,1,0:T(8,128)S(1)}, f32[64,4,8,128]{3,2,1,0:T(8,128)S(1)}, u32[]{:S(2)}, u32[]{:S(2)}) collective-permute-start(f32[64,4,8,128]{3,2,1,0:T(8,128)S(1)} %all_to_all.16.mine), channel_id=1, source_target_pairs={{0,4},{4,0},{1,5},{5,1},{2,6},{6,2},{3,7},{7,3},{8,12},{12,8},{9,1... | collective-permute-start | bytes 3145736 | tf_op jit(solution)/shard_map/ppermute | solution.py:228
  80.2 11.4 %collective-permute-start.2 = (f32[512,128]{1,0:T(8,128)S(1)}, f32[512,128]{1,0:T(8,128)}, u32[]{:S(2)}, u32[]{:S(2)}) collective-permute-start(f32[512,128]{1,0:T(8,128)S(1)} %copy-done.1), channel_id=1, source_target_pairs={{0,2},{1,3},{2,0},{3,1},{4,6},{5,7},{6,4},{7,5},{8,10},{9,11},{10,... | collective-permute-start | bytes 786440 | tf_op jit(solution)/shard_map/ppermute | solution.py:231
  83.0 14.6 %collective-permute-start.1 = (f32[512,128]{1,0:T(8,128)S(1)}, f32[512,128]{1,0:T(8,128)}, u32[]{:S(2)}, u32[]{:S(2)}) collective-permute-start(f32[512,128]{1,0:T(8,128)S(1)} %copy-done.1), channel_id=1, source_target_pairs={{0,1},{1,2},{2,3},{3,0},{4,5},{5,6},{6,7},{7,4},{8,9},{9,10},{10,1... | collective-permute-start | bytes 786440 | tf_op jit(solution)/shard_map/ppermute | solution.py:231
  85.5 12.1 %collective-permute-start.3 = (f32[512,128]{1,0:T(8,128)S(1)}, f32[512,128]{1,0:T(8,128)}, u32[]{:S(2)}, u32[]{:S(2)}) collective-permute-start(f32[512,128]{1,0:T(8,128)S(1)} %copy-done.1), channel_id=1, source_target_pairs={{0,3},{1,0},{2,1},{3,2},{4,7},{5,4},{6,5},{7,6},{8,11},{9,8},{10,9... | collective-permute-start | bytes 786440 | tf_op jit(solution)/shard_map/ppermute | solution.py:231
